TPU v7x, 256 devices: a whole 4x4x8 slice. The times are simulated.
256 devices in a mesh: ctx: 32 (over y, x, core), head: 4 (over z_lo), dp: 2 (over z_hi).
Axes of the slice: x: 4, y: 4, z: 8 (z_hi: 2, z_lo: 4; z = z_hi * 4 + z_lo), core: 2. Of those that a mesh axis runs over, the one named last changes fastest.
Arguments:
- queries: bfloat16 [2, 8192, 4096], P('dp', 'ctx', 'head'), may hold values from -6 to 6
- keys: bfloat16 [2, 8192, 4096], P('dp', 'ctx', 'head'), may hold values from -6 to 6
- values: bfloat16 [2, 8192, 4096], P('dp', 'ctx', 'head'), may hold values from -6 to 6
- log_decay: float32 [2, 32, 8192], P('dp', 'head', 'ctx'), may hold values from -1.5 to 0
- w_out: bfloat16 [128, 32, 3072], P(('ctx', 'dp'), 'head'), may hold values from -0.09375 to 0.09375
- grad_out: bfloat16 [2, 8192, 3072], P('dp', 'ctx'), may hold values from -6 to 6
Outputs:
- mixed: bfloat16 [2, 8192, 3072], P('dp', 'ctx', 'head')
- query_grad: bfloat16 [2, 8192, 4096], P('dp', 'ctx', 'head')
- key_grad: bfloat16 [2, 8192, 4096], P('dp', 'ctx', 'head')
- value_grad: bfloat16 [2, 8192, 4096], P('dp', 'ctx', 'head')
- w_grad: float32 [128, 32, 3072], P(('ctx', 'dp'), 'head')
All inputs are finite; a program needn't handle non-finite values.
Results may differ from a plain program's by a relative error of at most 0.015.
Values may be sent and summed in bfloat16 or wider, within the bound.
A program may use at most 128 MiB of HBM per device.

v0:
```python
import jax
import jax.numpy as jnp
from jax import lax
from jax.sharding import PartitionSpec as P

DH = 128
BLOCK = 256


def entering_2(array, axis, combine, identity, reverse):
    devices, mine = (lax.axis_size(axis), lax.axis_index(axis))
    everything = jax.tree.map(lambda part: lax.all_gather(part, axis), array)
    start = jax.tree.map(
        lambda part, zero: jnp.broadcast_to(jnp.asarray(zero, part.dtype), part.shape),
        array,
        identity,
    )

    def lap(k, before):
        at = devices - 1 - k if reverse else k
        reached = at > mine if reverse else at < mine
        new = combine(before, jax.tree.map(lambda part: part[at], everything))
        return jax.tree.map(lambda a, b: jnp.where(reached, a, b), new, before)

    return lax.fori_loop(0, devices, lap, start)


def block_weights(cumul):
    width = cumul.shape[-1]
    places = jnp.arange(width)
    lower = places[:, None] >= places[None, :]
    spread = cumul[..., :, None] - cumul[..., None, :]
    return jnp.exp(jnp.where(lower, spread, -jnp.inf))


def forward_join(earlier, later):
    return (earlier[0] * later[0], later[0][:, None, None] * earlier[1] + later[1])


def backward_combine(earlier, later):
    return (earlier[0] * later[0], later[1] + later[0][:, None, None] * earlier[1])


def shards(queries, keys, values, log_decay, w_out, grad_out):
    groups = log_decay.shape[1]
    length_here = queries.shape[1]
    tile_number = length_here // BLOCK
    scale = 1.0 / DH
    query_blocks = queries[0].reshape(tile_number, BLOCK, groups, DH)
    key_blocks = keys[0].reshape(tile_number, BLOCK, groups, DH)
    value_blocks = values[0].reshape(tile_number, BLOCK, groups, DH)
    places = jnp.arange(BLOCK)
    upper = (places[:, None] <= places[None, :]).astype(jnp.float32)
    cumul = jnp.einsum(
        "hnj,jt->hnt",
        log_decay[0].reshape(groups, tile_number, BLOCK),
        upper,
        precision=lax.Precision.HIGHEST,
    )
    weights = block_weights(cumul)
    decay_multiplier = jnp.transpose(scale * jnp.exp(cumul), (1, 2, 0))[..., None]
    tail = jnp.transpose(jnp.exp(cumul[..., -1:] - cumul), (1, 2, 0))[..., None]
    block_decay = jnp.exp(cumul[..., -1])
    ones_decay = jnp.ones((groups,), jnp.float32)
    zero_state = jnp.zeros((groups, DH, DH), jnp.float32)
    scores = jnp.einsum(
        "nthd,njhd->hntj", query_blocks, key_blocks, preferred_element_type=jnp.float32
    )
    probs = (scores * scale * weights).astype(jnp.bfloat16)
    intra = jnp.einsum("hntj,njhd->nthd", probs, value_blocks, preferred_element_type=jnp.float32)
    keys_weighted = (key_blocks * tail).astype(jnp.bfloat16)
    contrib = jnp.einsum(
        "nthd,nthe->hnde", keys_weighted, value_blocks, preferred_element_type=jnp.float32
    )
    total_decay = ones_decay
    total_state = zero_state
    index = 0
    total_state = block_decay[:, index][:, None, None] * total_state + contrib[:, index]
    total_decay = total_decay * block_decay[:, index]
    incoming = entering_2(
        (total_decay, total_state), "ctx", forward_join, (ones_decay, zero_state), False
    )[1]
    running = incoming
    index = 0
    entering = [running]
    state_low = jnp.stack(entering, axis=1).astype(jnp.bfloat16)
    inter = jnp.einsum(
        "nthd,hnde->nthe", query_blocks, state_low, preferred_element_type=jnp.float32
    )
    attended = (intra + inter * decay_multiplier).astype(jnp.bfloat16)
    attended_row_list = attended.reshape(length_here, groups, DH)
    panel = lax.all_gather(w_out, ("ctx", "dp"), axis=0, tiled=True)
    partial_out = jnp.einsum(
        "thd,dho->to", attended_row_list, panel, preferred_element_type=jnp.float32
    )
    mixed = lax.psum_scatter(
        partial_out.astype(jnp.bfloat16), "head", scatter_dimension=1, tiled=True
    )
    cotangent = grad_out[0]
    grad_heads = jnp.einsum(
        "to,dho->thd", cotangent, panel, preferred_element_type=jnp.float32
    ).astype(jnp.bfloat16)
    grad_blocks = grad_heads.reshape(tile_number, BLOCK, groups, DH)
    w_grad = lax.psum_scatter(
        jnp.einsum("thd,to->dho", attended_row_list, cotangent, preferred_element_type=jnp.float32),
        ("ctx", "dp"),
        scatter_dimension=0,
        tiled=True,
    )
    logit_gradient = jnp.einsum(
        "nthe,njhe->hntj", grad_blocks, value_blocks, preferred_element_type=jnp.float32
    )
    dprobs = (logit_gradient * scale * weights).astype(jnp.bfloat16)
    queries_weighted = (query_blocks * decay_multiplier).astype(jnp.bfloat16)
    local_grad = jnp.einsum(
        "nthd,nthe->hnde", queries_weighted, grad_blocks, preferred_element_type=jnp.float32
    )
    faded_carry = ones_decay
    after_state = zero_state
    for index in reversed(range(tile_number)):
        after_state = block_decay[:, index][:, None, None] * after_state + local_grad[:, index]
        faded_carry = faded_carry * block_decay[:, index]
    leaving = entering_2(
        (faded_carry, after_state), "ctx", backward_combine, (ones_decay, zero_state), True
    )[1]
    exiting = []
    running = leaving
    for index in reversed(range(tile_number)):
        exiting = [running] + exiting
        running = block_decay[:, index][:, None, None] * running + local_grad[:, index]
    back_low = jnp.stack(exiting, axis=1).astype(jnp.bfloat16)
    query_grad = (
        jnp.einsum("hntj,njhd->nthd", dprobs, key_blocks, preferred_element_type=jnp.float32)
        + jnp.einsum("nthe,hnde->nthd", grad_blocks, state_low, preferred_element_type=jnp.float32)
        * decay_multiplier
    )
    key_grad = jnp.einsum(
        "hntj,nthd->njhd", dprobs, query_blocks, preferred_element_type=jnp.float32
    ) + tail * jnp.einsum(
        "nthe,hnde->nthd", value_blocks, back_low, preferred_element_type=jnp.float32
    )
    value_grad = jnp.einsum(
        "hntj,nthe->njhe", probs, grad_blocks, preferred_element_type=jnp.float32
    ) + tail * jnp.einsum(
        "nthd,hnde->nthe", key_blocks, back_low, preferred_element_type=jnp.float32
    )
    flat = (1, length_here, groups * DH)
    return (
        mixed[None],
        query_grad.astype(jnp.bfloat16).reshape(flat),
        key_grad.astype(jnp.bfloat16).reshape(flat),
        value_grad.astype(jnp.bfloat16).reshape(flat),
        w_grad,
    )


def solution(mesh):
    return jax.shard_map(
        shards,
        mesh=mesh,
        in_specs=(
            P("dp", "ctx", "head"),
            P("dp", "ctx", "head"),
            P("dp", "ctx", "head"),
            P("dp", "head", "ctx"),
            P(("ctx", "dp"), "head", None),
            P("dp", "ctx", None),
        ),
        out_specs=(
            P("dp", "ctx", "head"),
            P("dp", "ctx", "head"),
            P("dp", "ctx", "head"),
            P("dp", "ctx", "head"),
            P(("ctx", "dp"), "head", None),
        ),
        check_vma=False,
    )
```

profile of v0, /device:TPU:1, one launch (start us, length us, event | category | flops | bytes accessed | tf_op | source)
XLA Modules:
  0.0 551.8 jit_solution(11020169705880743914)
XLA Ops:
  9.1 1.3 copy.96
  12.5 1.2 copy.94
  13.7 104.7 %all-gather.7.cloned.1.call-done = bf16[128,8,3072]{2,1,0:T(8,128)(2,1)} async-done(((bf16[2,8,3072]{2,1,0:T(8,128)(2,1)}), bf16[128,8,3072]{2,1,0:T(8,128)(2,1)}) %all-gather.7.cloned.1.call-update) | async-done | bytes 6291472 | tf_op jit(solution)/shard_map/all_gather | solution.py:92
  118.4 4.6 fusion.11
  126.6 63.6 %all-reduce = f32[256]{0:T(256)S(1)} all-reduce(f32[256]{0:T(256)S(1)} %dynamic-update-slice), channel_id=2, replica_groups=mesh['ctx'=32,'head'=4,'dp'=2] {'ctx'}, use_global_device_ids=true, to_apply=%add | all-reduce | flops 256 | bytes 2048
  190.3 1.8 multiply_convert_fusion.1
  193.1 1.4 convolution_bitcast_fusion.8
  194.5 39.3 %while.30 = (s32[]{:T(128)}, f32[8,128,128]{2,1,0:T(8,128)S(1)}, s32[]{:T(128)}, f32[32,8]{1,0:T(8,128)S(1)}, f32[32,8,128,128]{3,2,1,0:T(8,128)}, /*index=5*/s32[]{:T(128)}, s32[]{:T(128)}) while((s32[]{:T(128)}, f32[8,128,128]{2,1,0:T(8,128)S(1)}, s32[]{:T(128)}, f32[32,8]{1,0:T(8,128)S(1)}, f32[32,8,128,128]{3,2,1,0:T(8,128)}, ...), condition=%wide.region_1.2_spmd.clone, body=%wide.region_0.1_spmd.clone.sunk | while | flops 524292 | bytes 1573073 | solution.py:25
  205.5 1.2 fusion.58
  206.7 1.2 fusion.58
  208.0 1.3 fusion.58
  211.7 1.2 fusion.58
  212.9 1.2 fusion.58
  214.2 1.2 fusion.58
  216.6 1.2 fusion.58
  232.5 1.3 fusion.58
  233.8 1.9 fusion.25
  236.5 17.9 %fusion.7 = bf16[256,3072]{1,0:T(8,128)(2,1)} fusion(bf16[256,8,128]{2,0,1:T(8,128)(2,1)S(1)} %fusion.25, bf16[128,8,3072]{2,1,0:T(8,128)(2,1)} %all-gather.7.cloned.1.call-done), kind=kOutput, calls=%fused_computation.10 | convolution fusion | flops 1611399168 | bytes 8388608 | tf_op jit(solution)/shard_map/thd,dho->to/dot_general | solution.py:93
  255.5 6.4 %convolution_bitcast_fusion = f32[128,8,3072]{2,0,1:T(8,128)} fusion(bf16[256,8,128]{2,0,1:T(8,128)(2,1)S(1)} %copy-done.10, bf16[1,256,3072]{2,1,0:T(8,128)(2,1)S(1)} %copy-done), kind=kOutput, calls=%fused_computation.6 | convolution fusion | flops 1610612736 | bytes 14680064 | tf_op jit(solution)/shard_map/thd,to->dho/dot_general | solution.py:105
  261.9 16.7 %copy.81 = f32[128,8,3072]{2,1,0:T(8,128)} copy(f32[128,8,3072]{2,0,1:T(8,128)} %convolution_bitcast_fusion) | data formatting | bytes 25165824 | tf_op jit(solution)/shard_map/thd,to->dho/transpose | solution.py:105
  280.7 1.3 convolution_bitcast_fusion.5
  282.4 1.3 convolution_bitcast_fusion.6
  285.9 39.4 %while.31 = (s32[]{:T(128)}, f32[8,128,128]{2,1,0:T(8,128)S(1)}, s32[]{:T(128)}, f32[32,8,128,128]{3,2,1,0:T(8,128)}, f32[32,8]{1,0:T(8,128)S(1)}, /*index=5*/s32[]{:T(128)}, s32[]{:T(128)}, s32[]{:T(128)}, s32[]{:T(128)}) while((s32[]{:T(128)}, f32[8,128,128]{2,1,0:T(8,128)S(1)}, s32[]{:T(128)}, f32[32,8,128,128]{3,2,1,0:T(8,128)}, ...), condition=%wide.region_4.5_spmd.clone, body=%wide.region_3.4_spmd.clone.sunk | while | flops 524296 | bytes 1573135 | solution.py:25
  285.9 1.3 fusion.59
  293.4 1.2 fusion.59
  295.8 1.2 fusion.59
  304.4 1.2 fusion.59
  308.1 1.2 fusion.59
  314.3 1.2 fusion.59
  326.4 2.2 copy.83
  328.6 1.6 fusion.22
  331.2 214.1 %reduce-scatter.5.cloned.1.call-done = f32[2,8,3072]{2,1,0:T(8,128)} async-done(((f32[128,8,3072]{2,1,0:T(8,128)}), f32[2,8,3072]{2,1,0:T(8,128)}) %reduce-scatter.5.cloned.1.call-update) | async-done | bytes 196624 | tf_op jit(solution)/shard_map/reduce_scatter | solution.py:104
  (184 shorter events, 75.7 us)
Async XLA Ops:
  7.2 111.3 %copy-start = (bf16[1,256,3072]{2,1,0:T(8,128)(2,1)S(1)}, bf16[1,256,3072]{2,1,0:T(8,128)(2,1)}, u32[]{:S(2)}) copy-start(bf16[1,256,3072]{2,1,0:T(8,128)(2,1)} %param.15) | copy-start | bytes 4718596
  7.2 3.6 copy-start.16
  7.2 111.2 %all-gather.7.cloned.1.call-start = ((), (), s32[]{:S(2)}) async-start(), calls=%async_computation.2 | async-start | bytes 6389760 | tf_op jit(solution)/shard_map/all_gather | solution.py:92
  7.9 186.6 %all-gather.9.cloned.1.call-start = ((), (), s32[]{:S(2)}) async-start(), calls=%async_computation.5 | async-start | bytes 17301504 | tf_op jit(solution)/shard_map/all_gather | solution.py:12
  9.1 3.3 copy-start.4
  10.8 1.6 copy-start.14
  12.4 273.4 %all-gather.11.cloned.1.call-start = ((), (), s32[]{:S(2)}) async-start(), calls=%async_computation.6 | async-start | bytes 17301504 | tf_op jit(solution)/shard_map/all_gather | solution.py:12
  13.7 220.1 %copy-start.2 = (bf16[1,256,1024]{1,2,0:T(8,128)(2,1)}, bf16[1,256,1024]{1,2,0:T(8,128)(2,1)S(1)}, u32[]{:S(2)}) copy-start(bf16[1,256,1024]{1,2,0:T(8,128)(2,1)S(1)} %copy.94) | copy-start | bytes 1572868
  123.0 0.8 copy-start.11
  123.0 2.0 copy-start.17
  125.0 206.2 %reduce-scatter.3.cloned.1.call-start = ((), (), s32[]{:S(2)}) async-start(), calls=%async_computation.3 | async-start | bytes 1966080 | tf_op jit(solution)/shard_map/reduce_scatter | solution.py:96
  192.1 1.0 copy-start.6
  235.7 0.8 copy-start.9
  254.4 1.1 copy-start.10
  254.5 290.8 %reduce-scatter.5.cloned.1.call-start = ((), (), s32[]{:S(2)}) async-start(), calls=%async_computation.4 | async-start | bytes 12779520 | tf_op jit(solution)/shard_map/reduce_scatter | solution.py:104
  278.6 1.0 copy-start.12
  279.6 1.0 copy-start.3
  280.7 1.3 copy-start.7
  280.7 1.7 copy-start.13
  280.7 3.0 copy-start.15
  285.9 39.4 %copy-start.8 = (f32[1,256,8,128]{1,3,2,0:T(8,128)S(1)}, f32[1,256,8,128]{1,3,2,0:T(8,128)}, u32[]{:S(2)}) copy-start(f32[1,256,8,128]{1,3,2,0:T(8,128)} %convolution_bitcast_fusion.5) | copy-start | bytes 3145732
  325.3 3.3 copy-start.5
  326.4 218.8 %copy-start.1 = (bf16[1,256,3072]{2,1,0:T(8,128)(2,1)S(1)}, bf16[1,256,3072]{2,1,0:T(8,128)(2,1)}, u32[]{:S(2)}) copy-start(bf16[1,256,3072]{2,1,0:T(8,128)(2,1)} %param.15) | copy-start | bytes 4718596
Sparse Core Ops, SparseCore 0:
  11.8 106.5 all-gather.6
  121.5 71.6 all-gather.8
  195.8 76.6 all-gather.10
  275.5 39.5 reduce-scatter.2
  321.7 223.4 reduce-scatter.4
where the time goes:
time: 555 us; the launch traced here: 552 us
  waiting for transfers between devices  320 us (58%)
  other arithmetic  76 us (14%)
  blocking collectives  63.6 us (11%)
  matrix products  43.5 us (8%)
  local copies, waits for them, and re-layouts  31.6 us (6%)
  between operations  14.7 us (3%)
    reduce_scatter x1, waiting for transfers between devices, shards(): lax.psum_scatter(jnp.einsum('thd,to->dho', attended_row_list, cotangent,...  214 us
    all_gather x1, waiting for transfers between devices, shards(): panel = lax.all_gather(w_out, ('ctx', 'dp'), axis=0, tiled=True)  105 us
    select_n x64, other arithmetic, lap(): return jax.tree.map(lambda a, b: jnp.where(reached, a, b), new, before)  75.7 us
    unnamed x1, blocking collectives  63.6 us
    dot_general x1, matrix products, shards(): jnp.einsum('thd,dho->to', attended_row_list, panel, preferred_element_typ...  17.9 us
    transpose x1, local copies, waits for them, and re-layouts, shards(): jnp.einsum('thd,to->dho', attended_row_list, cotangent, preferred_element...  16.7 us
    unnamed x44, local copies, waits for them, and re-layouts  12.5 us
  transfers between devices with their start and end apart: 5, of which 2 were waited for; matrix products, arithmetic and copies ran while one was open for 26% of the time, Pallas kernels for 0%

commit v1 on v0

v1 whole, which is shorter than its diff:
```python
import jax
import jax.numpy as jnp
from jax import lax
from jax.experimental import pallas as pl
from jax.experimental.pallas import tpu as pltpu
from jax.sharding import PartitionSpec as P

DH = 128
BLOCK = 256
HEADS = 8
DOUT = 3072
HALF = DOUT // 2
CTX = 32
SCALE = 1.0 / DH
F32 = jnp.float32
BF16 = jnp.bfloat16
NT = (((1,), (1,)), ((), ()))
NN = (((1,), (0,)), ((), ()))
TN = (((0,), (0,)), ((), ()))


def mm(a, b, dims):
    return lax.dot_general(a, b, dims, preferred_element_type=F32)


class Ids:
    def __init__(self):
        self.names = {}

    def __call__(self, *name):
        return self.names.setdefault(name, len(self.names))


def kernel(
    q_ref, k_ref, v_ref, ld_ref, w_ref, go_ref,
    mixed_ref, qg_ref, kg_ref, vg_ref, wg_ref,
    panel, pt, cum, ccol, probs, intra, kpart, vpart, att, attp, gh,
    cf, rf, ef, low, cb, rb, eb, back,
    go_sib, att_t, att_sib,
    wp, wacc, xb, yb, wa, xa, ya, xz,
    mp, macc, mr1, mr2,
    ssem, rsem, a2a_s, a2a_r,
):
    ctx, head, dp = lax.axis_index("ctx"), lax.axis_index("head"), lax.axis_index("dp")
    core = ctx % 2
    x, y = (ctx // 2) % 4, ctx // 8
    a = x * (1 - core) + y * core
    b = y * (1 - core) + x * core
    ap, am, ao = (a + 1) % 4, (a + 3) % 4, (a + 2) % 4
    bp, bm, bo = (b + 1) % 4, (b + 3) % 4, (b + 2) % 4
    z, zo = dp, 1 - dp

    def at(a1, b1):
        x1 = a1 * (1 - core) + b1 * core
        y1 = b1 * (1 - core) + a1 * core
        return ((y1 * 4 + x1) * 2 + core, head, dp)

    dev_ap, dev_am, dev_bp, dev_bm = at(ap, b), at(am, b), at(a, bp), at(a, bm)
    dev_sib = (ctx + 1 - 2 * core, head, dp)
    dev_z = (ctx, head, zo)
    h1 = head + 1 - 2 * (head % 2)
    h2 = (head + 2) % 4
    h3 = (h1 + 2) % 4
    dev_h1, dev_h2 = (ctx, h1, dp), (ctx, h2, dp)

    ids = Ids()
    started = []

    def xfer(name, src, dst, dev):
        i = ids(*name)
        return pltpu.make_async_remote_copy(
            src_ref=src, dst_ref=dst, send_sem=ssem.at[i], recv_sem=rsem.at[i],
            device_id=dev, device_id_type=pl.DeviceIdType.MESH,
        )

    def send(name, src, dst, dev):
        copy = xfer(name, src, dst, dev)
        copy.start()
        started.append(copy)

    def recv(name, ref, dev):
        xfer(name, ref, ref, dev).wait_recv()

    barrier = pltpu.get_barrier_semaphore()

    def greet(i, carry):
        pl.semaphore_signal(
            barrier, inc=1, device_id=((ctx + i) % CTX, head, dp), device_id_type=pl.DeviceIdType.MESH
        )
        return carry

    lax.fori_loop(1, CTX, greet, 0)
    for dev in (dev_z, dev_h1, dev_h2):
        pl.semaphore_signal(barrier, inc=1, device_id=dev, device_id_type=pl.DeviceIdType.MESH)
    pl.semaphore_wait(barrier, CTX - 1 + 3)

    def slot(a1, b1, z1):
        return core * 32 + b1 * 8 + a1 * 2 + z1

    def whole(s):
        return panel.at[s]

    def part(s, h):
        return panel.at[s, :, pl.ds(h * HALF, HALF)]

    a_of = {0: a, 1: am, 2: ap, 3: ao}

    def b_sends(zi, k):
        zz = (z, zo)[zi]
        ref = whole(slot(a_of[k], b, zz))
        send(("bp", zi, k), ref, ref, dev_bp)
        send(("bm", zi, k), ref, ref, dev_bm)

    def a_sends(zi):
        ref = whole(slot(a, b, (z, zo)[zi]))
        send(("ap", zi), ref, ref, dev_ap)
        send(("am", zi), ref, ref, dev_am)

    def step_a(zi):
        zz = (z, zo)[zi]
        left, right = slot(am, b, zz), slot(ap, b, zz)
        recv(("ap", zi), whole(left), dev_am)
        send(("afp", zi), part(left, 0), part(left, 0), dev_ap)
        b_sends(zi, 1)
        recv(("am", zi), whole(right), dev_ap)
        send(("afm", zi), part(right, 1), part(right, 1), dev_am)
        b_sends(zi, 2)

    def step_ao(zi):
        far = slot(ao, b, (z, zo)[zi])
        recv(("afp", zi), part(far, 0), dev_am)
        recv(("afm", zi), part(far, 1), dev_ap)
        b_sends(zi, 3)

    def step_b(zi, k):
        zz = (z, zo)[zi]
        below, above = slot(a_of[k], bm, zz), slot(a_of[k], bp, zz)
        recv(("bp", zi, k), whole(below), dev_bm)
        send(("bfp", zi, k), part(below, 0), part(below, 0), dev_bp)
        recv(("bm", zi, k), whole(above), dev_bp)
        send(("bfm", zi, k), part(above, 1), part(above, 1), dev_bm)

    def step_bo(zi, k):
        far = slot(a_of[k], bo, (z, zo)[zi])
        recv(("bfp", zi, k), part(far, 0), dev_bm)
        recv(("bfm", zi, k), part(far, 1), dev_bp)

    def step_z():
        recv(("z",), whole(slot(a, b, zo)), dev_z)
        a_sends(1)
        b_sends(1, 0)

    def row(c1, b1):
        return panel.at[pl.ds(c1 * 32 + b1 * 8, 8)]

    def sib_send(k):
        ref = row(core, (b, bm, bp, bo)[k])
        send(("sib", k), ref, ref, dev_sib)

    def sib_recv(k):
        recv(("sib", k), row(1 - core, (a, am, ap, ao)[k]), dev_sib)

    mine = slot(a, b, z)
    panel[mine] = w_ref[...]
    send(("z",), whole(mine), whole(mine), dev_z)
    a_sends(0)
    b_sends(0, 0)
    send(("go",), go_ref, go_sib, dev_sib)

    t_row = lax.broadcasted_iota(jnp.int32, (BLOCK, BLOCK), 0)
    t_col = lax.broadcasted_iota(jnp.int32, (BLOCK, BLOCK), 1)
    upper = (t_row <= t_col).astype(F32)
    cum[...] = jnp.dot(ld_ref[...], upper, precision=lax.Precision.HIGHEST, preferred_element_type=F32)

    def lanes(h):
        return pl.ds(pl.multiple_of(h * DH, DH), DH)

    def weights(h):
        col = ccol[h]
        spread = jnp.concatenate([col, col], axis=1) - cum[pl.ds(h, 1), :]
        rows = lax.broadcasted_iota(jnp.int32, (BLOCK, BLOCK), 0)
        cols = lax.broadcasted_iota(jnp.int32, (BLOCK, BLOCK), 1)
        return jnp.exp(jnp.where(rows >= cols, spread, -jnp.inf))

    def pieces(buf, h, total, decay):
        for r in range(4):
            buf[h * 4 + r, 0:32, :] = total[r * 32 : (r + 1) * 32]
            buf[h * 4 + r, 32:40, :] = jnp.broadcast_to(decay, (8, DH))

    def fwd_share(h, carry):
        wide = jnp.broadcast_to(cum[pl.ds(h, 1), :], (DH, BLOCK))
        col = wide.T
        ccol[h] = col
        last = col[BLOCK - 1 : BLOCK, :]
        kw = (k_ref[:, lanes(h)].astype(F32) * jnp.exp(last - col)).astype(BF16)
        pieces(cf, h, mm(kw, v_ref[:, lanes(h)], TN), jnp.exp(last))
        return carry

    lax.fori_loop(0, HEADS, fwd_share, 0)

    def a2a(n, src, dst, i, out):
        other = (ctx + i) % CTX if out else (ctx + CTX - i) % CTX
        return pltpu.make_async_remote_copy(
            src_ref=src.at[other], dst_ref=dst.at[ctx if out else other],
            send_sem=a2a_s.at[n, i], recv_sem=a2a_r.at[n, i],
            device_id=(other, head, dp), device_id_type=pl.DeviceIdType.MESH,
        )

    def a2a_start(n, src, dst):
        def go(i, carry):
            a2a(n, src, dst, i, True).start()
            return carry

        lax.fori_loop(1, CTX, go, 0)
        dst[ctx] = src[ctx]

    def a2a_recv(n, src, dst):
        def go(i, carry):
            a2a(n, src, dst, i, False).wait_recv()
            return carry

        lax.fori_loop(1, CTX, go, 0)

    def a2a_sent(n, src, dst):
        def go(i, carry):
            a2a(n, src, dst, i, True).wait_send()
            return carry

        lax.fori_loop(1, CTX, go, 0)

    def scan(got, out, reverse):
        def go(i, state):
            at_block = CTX - 1 - i if reverse else i
            out[at_block] = state.astype(BF16)
            return state * got[at_block, 32:33, :] + got[at_block, 0:32, :]

        lax.fori_loop(0, CTX, go, jnp.zeros((32, DH), F32))

    def state_of(buf, h):
        return buf[pl.ds(h * 4, 4)].reshape(DH, DH)

    a2a_start(0, cf, rf)
    step_a(0)
    step_z()

    def inside(h, carry):
        scores = mm(q_ref[:, lanes(h)], k_ref[:, lanes(h)], NT)
        p = (scores * SCALE * weights(h)).astype(BF16)
        probs[h] = p
        intra[:, lanes(h)] = mm(p, v_ref[:, lanes(h)], NN)
        return carry

    lax.fori_loop(0, HEADS // 2, inside, 0)
    step_ao(0)
    step_b(0, 0)
    step_a(1)
    lax.fori_loop(HEADS // 2, HEADS, inside, 0)
    a2a_recv(0, cf, rf)
    scan(rf, ef, False)
    a2a_start(1, ef, low)
    step_b(0, 1)
    step_b(0, 2)
    step_ao(1)
    step_b(1, 0)
    sib_send(0)

    r = lax.broadcasted_iota(jnp.int32, (1024, DH), 0)
    place = r >> 4
    pc, pb, pa, pz = place >> 5, (place >> 3) & 3, (place >> 1) & 3, place & 1
    px = jnp.where(pc == 0, pa, pb)
    py = jnp.where(pc == 0, pb, pa)
    feature = 2 * ((((py * 4) + px) * 2 + pc) * 2 + pz) + ((r >> 3) & 1)
    lane = lax.broadcasted_iota(jnp.int32, (1024, DH), 1)
    same = feature == lane
    for h in range(HEADS):
        pt[:, h * DH : (h + 1) * DH] = jnp.where(same & ((r & 7) == h), 1.0, 0.0).astype(BF16)

    step_b(0, 3)
    step_b(1, 1)
    step_b(1, 2)

    a2a_recv(1, ef, low)

    def attend(h, carry):
        inter = mm(q_ref[:, lanes(h)], state_of(low, h), NN)
        factor = SCALE * jnp.exp(ccol[h])
        att[:, lanes(h)] = (intra[:, lanes(h)] + inter * factor).astype(BF16)
        return carry

    lax.fori_loop(0, HEADS, attend, 0)
    step_b(1, 3)
    sib_send(1)
    sib_send(2)

    def turn(i, carry):
        rows = pl.ds(pl.multiple_of(i * 256, 256), 256)
        att_t[rows, :] = mm(pt[rows, :], att[...], NT).astype(BF16)
        attp[:, rows] = mm(att[...], pt[rows, :], NT).astype(BF16)
        return carry

    lax.fori_loop(0, 4, turn, 0)
    other_rows = pl.ds(pl.multiple_of((1 - core) * 512, 512), 512)
    send(("att",), att_t.at[other_rows], att_sib, dev_sib)
    for zi in range(2):
        for k in range(4):
            step_bo(zi, k)
    sib_send(3)

    for k in range(4):
        sib_recv(k)

    def heads_grad(i, carry):
        rows = panel[pl.ds(i * 16, 16)].reshape(256, DOUT)
        attp_cols = pl.ds(pl.multiple_of(i * 256, 256), 256)
        gh[:, attp_cols] = mm(go_ref[...], rows, NT).astype(BF16)
        return carry

    lax.fori_loop(0, 4, heads_grad, 0)
    by_head = []
    for n in range(4):
        by_head.append(mm(gh[...], pt[:, n * 256 : (n + 1) * 256], NN).astype(BF16))
    for n in range(4):
        gh[:, n * 256 : (n + 1) * 256] = by_head[n]

    def bwd_share(h, carry):
        qw = (q_ref[:, lanes(h)].astype(F32) * (SCALE * jnp.exp(ccol[h]))).astype(BF16)
        last = ccol[h, BLOCK - 1 : BLOCK, :]
        pieces(cb, h, mm(qw, gh[:, lanes(h)], TN), jnp.exp(last))
        return carry

    lax.fori_loop(0, HEADS, bwd_share, 0)
    a2a_start(2, cb, rb)

    def mix(dest, store):
        def go(n, carry):
            cols = pl.ds(pl.multiple_of(dest * 768 + n * 256, 256), 256)
            w = panel[:, :, cols].reshape(1024, 256)
            store(pl.ds(pl.multiple_of(n * 256, 256), 256), mm(attp[...], w, NN))
            return carry

        lax.fori_loop(0, 3, go, 0)

    def store_at(dest):
        def store(cols, value):
            mp[dest, :, cols] = value.astype(BF16)

        return store

    def store_own(cols, value):
        macc[:, cols] = value

    mix(h3, store_at(h3))
    send(("m", 0), mp.at[h3], mr1.at[0], dev_h1)
    mix(h1, store_at(h1))
    send(("m", 1), mp.at[h1], mr1.at[1], dev_h1)

    recv(("go",), go_sib, dev_sib)
    recv(("att",), att_sib, dev_sib)

    def w_rows(b1, n):
        cols = pl.ds(pl.multiple_of(n * 256, 256), 256)
        own = att_t[pl.ds(pl.multiple_of(core * 512 + b1 * 128, 128), 128), :]
        sib = att_sib[pl.ds(pl.multiple_of(b1 * 128, 128), 128), :]
        return cols, mm(own, go_ref[:, cols], NN) + mm(sib, go_sib[:, cols], NN)

    def w_block(b1):
        def go(n, carry):
            cols, value = w_rows(b1, n)
            wp[b1, :, cols] = value.astype(BF16)
            return carry

        lax.fori_loop(0, 12, go, 0)

    def w_own(n, carry):
        cols, value = w_rows(b, n)
        wacc[:, cols] = value
        return carry

    lo, hi = pl.ds(0, HALF), pl.ds(HALF, HALF)
    w_block(bo)
    send(("w", 0), wp.at[bo, :, lo], xb.at[0], dev_bp)
    send(("w", 1), wp.at[bo, :, hi], xb.at[1], dev_bm)
    w_block(bp)
    send(("w", 2), wp.at[bp, :, hi], yb.at[0, :, hi], dev_bp)
    w_block(bm)
    send(("w", 3), wp.at[bm, :, lo], yb.at[1, :, lo], dev_bm)
    lax.fori_loop(0, 12, w_own, 0)
    mix(h2, store_at(h2))
    mix(head, store_own)

    def grads(h, carry):
        g, kk, vv, qq = gh[:, lanes(h)], k_ref[:, lanes(h)], v_ref[:, lanes(h)], q_ref[:, lanes(h)]
        dp_h = (mm(g, vv, NT) * SCALE * weights(h)).astype(BF16)
        factor = SCALE * jnp.exp(ccol[h])
        qg = mm(dp_h, kk, NN) + mm(g, state_of(low, h), NT) * factor
        qg_ref[:, lanes(h)] = qg.astype(BF16)
        kpart[:, lanes(h)] = mm(dp_h, qq, TN)
        vpart[:, lanes(h)] = mm(probs[h], g, TN)
        return carry

    def widen(ref):
        return ref.astype(F32)

    lax.fori_loop(0, 2, grads, 0)
    a2a_recv(2, cb, rb)
    scan(rb, eb, True)
    a2a_start(3, eb, back)

    recv(("w", 0), xb.at[0], dev_bm)
    wp[bp, :, lo] = (widen(wp[bp, :, lo]) + widen(xb[0])).astype(BF16)
    send(("w", 4), wp.at[bp, :, lo], yb.at[0, :, lo], dev_bp)
    recv(("w", 1), xb.at[1], dev_bp)
    wp[bm, :, hi] = (widen(wp[bm, :, hi]) + widen(xb[1])).astype(BF16)
    send(("w", 5), wp.at[bm, :, hi], yb.at[1, :, hi], dev_bm)

    lax.fori_loop(2, 5, grads, 0)
    recv(("m", 0), mr1.at[0], dev_h1)
    mp[h2] = (widen(mp[h2]) + widen(mr1[0])).astype(BF16)
    send(("m", 2), mp.at[h2], mr2, dev_h2)
    lax.fori_loop(5, HEADS, grads, 0)

    recv(("w", 2), yb.at[0, :, hi], dev_bm)
    recv(("w", 3), yb.at[1, :, lo], dev_bp)
    recv(("w", 4), yb.at[0, :, lo], dev_bm)
    recv(("w", 5), yb.at[1, :, hi], dev_bp)

    def w_sum(n, carry):
        cols = pl.ds(pl.multiple_of(n * 256, 256), 256)
        total = wacc[:, cols] + widen(yb[0, :, cols]) + widen(yb[1, :, cols])
        wacc[:, cols] = total
        wa[:, cols] = total.astype(BF16)
        return carry

    lax.fori_loop(0, 12, w_sum, 0)

    def rows_of(a1):
        return pl.ds(pl.multiple_of(a1 * 32, 32), 32)

    send(("v", 0), wa.at[rows_of(ao), lo], xa.at[0], dev_ap)
    send(("v", 1), wa.at[rows_of(ao), hi], xa.at[1], dev_am)
    send(("v", 2), wa.at[rows_of(ap), hi], ya.at[0, :, hi], dev_ap)
    send(("v", 3), wa.at[rows_of(am), lo], ya.at[1, :, lo], dev_am)

    a2a_recv(3, eb, back)

    def finish(h, carry):
        col = ccol[h]
        tail = jnp.exp(col[BLOCK - 1 : BLOCK, :] - col)
        state = state_of(back, h)
        kg = kpart[:, lanes(h)] + tail * mm(v_ref[:, lanes(h)], state, NT)
        vg = vpart[:, lanes(h)] + tail * mm(k_ref[:, lanes(h)], state, NN)
        kg_ref[:, lanes(h)] = kg.astype(BF16)
        vg_ref[:, lanes(h)] = vg.astype(BF16)
        return carry

    lax.fori_loop(0, HEADS, finish, 0)

    recv(("v", 0), xa.at[0], dev_am)
    wa[rows_of(ap), lo] = (widen(wa[rows_of(ap), lo]) + widen(xa[0])).astype(BF16)
    send(("v", 4), wa.at[rows_of(ap), lo], ya.at[0, :, lo], dev_ap)
    recv(("v", 1), xa.at[1], dev_ap)
    wa[rows_of(am), hi] = (widen(wa[rows_of(am), hi]) + widen(xa[1])).astype(BF16)
    send(("v", 5), wa.at[rows_of(am), hi], ya.at[1, :, hi], dev_am)
    recv(("v", 2), ya.at[0, :, hi], dev_am)
    recv(("v", 3), ya.at[1, :, lo], dev_ap)
    recv(("v", 4), ya.at[0, :, lo], dev_am)
    recv(("v", 5), ya.at[1, :, hi], dev_ap)

    def own_rows(z1):
        return pl.ds(pl.multiple_of(a * 32 + z1 * 16, 16), 16)

    def from_both(z1):
        rows = pl.ds(pl.multiple_of(z1 * 16, 16), 16)
        return wacc[own_rows(z1), :] + widen(ya[0, rows, :]) + widen(ya[1, rows, :])

    wa[own_rows(zo), :] = from_both(zo).astype(BF16)
    send(("v", 6), wa.at[own_rows(zo)], xz, dev_z)
    wg_ref[...] = from_both(z)

    recv(("m", 1), mr1.at[1], dev_h1)
    recv(("m", 2), mr2, dev_h2)
    mixed_ref[...] = (macc[...] + widen(mr1[1]) + widen(mr2[...])).astype(BF16)

    recv(("v", 6), xz, dev_z)
    wg_ref[...] += widen(xz[...])

    for copy in started:
        copy.wait_send()
    for n, src, dst in ((0, cf, rf), (1, ef, low), (2, cb, rb), (3, eb, back)):
        a2a_sent(n, src, dst)


def shards(queries, keys, values, log_decay, w_out, grad_out):
    vmem = pl.BlockSpec(memory_space=pltpu.VMEM)
    length = queries.shape[1]
    features = HEADS * DH

    def buf(shape, dtype):
        return pltpu.VMEM(shape, dtype)

    mixed, qg, kg, vg, wg = pl.pallas_call(
        kernel,
        out_shape=(
            jax.ShapeDtypeStruct((length, DOUT // 4), BF16),
            jax.ShapeDtypeStruct((length, features), BF16),
            jax.ShapeDtypeStruct((length, features), BF16),
            jax.ShapeDtypeStruct((length, features), BF16),
            jax.ShapeDtypeStruct((16, DOUT), F32),
        ),
        in_specs=[vmem] * 6,
        out_specs=(vmem,) * 5,
        scratch_shapes=[
            buf((64, 16, DOUT), BF16),
            buf((features, features), BF16),
            buf((HEADS, BLOCK), F32),
            buf((HEADS, BLOCK, DH), F32),
            buf((HEADS, BLOCK, BLOCK), BF16),
            buf((BLOCK, features), F32),
            buf((BLOCK, features), F32),
            buf((BLOCK, features), F32),
            buf((BLOCK, features), BF16),
            buf((BLOCK, features), BF16),
            buf((BLOCK, features), BF16),
            buf((CTX, 40, DH), F32),
            buf((CTX, 40, DH), F32),
            buf((CTX, 32, DH), BF16),
            buf((CTX, 32, DH), BF16),
            buf((CTX, 40, DH), F32),
            buf((CTX, 40, DH), F32),
            buf((CTX, 32, DH), BF16),
            buf((CTX, 32, DH), BF16),
            buf((BLOCK, DOUT), BF16),
            buf((features, BLOCK), BF16),
            buf((512, BLOCK), BF16),
            buf((4, 128, DOUT), BF16),
            buf((128, DOUT), F32),
            buf((2, 128, HALF), BF16),
            buf((2, 128, DOUT), BF16),
            buf((128, DOUT), BF16),
            buf((2, 32, HALF), BF16),
            buf((2, 32, DOUT), BF16),
            buf((16, DOUT), BF16),
            buf((4, BLOCK, 768), BF16),
            buf((BLOCK, 768), F32),
            buf((2, BLOCK, 768), BF16),
            buf((BLOCK, 768), BF16),
            pltpu.SemaphoreType.DMA((72,)),
            pltpu.SemaphoreType.DMA((72,)),
            pltpu.SemaphoreType.DMA((4, CTX)),
            pltpu.SemaphoreType.DMA((4, CTX)),
        ],
        compiler_params=pltpu.CompilerParams(
            collective_id=0, has_side_effects=True, vmem_limit_bytes=60 * 1024 * 1024
        ),
        name="step",
    )(queries[0], keys[0], values[0], log_decay[0], w_out.reshape(16, DOUT), grad_out[0])
    return mixed[None], qg[None], kg[None], vg[None], wg.reshape(2, HEADS, DOUT)


def solution(mesh):
    return jax.shard_map(
        shards,
        mesh=mesh,
        in_specs=(
            P("dp", "ctx", "head"),
            P("dp", "ctx", "head"),
            P("dp", "ctx", "head"),
            P("dp", "head", "ctx"),
            P(("ctx", "dp"), "head", None),
            P("dp", "ctx", None),
        ),
        out_specs=(
            P("dp", "ctx", "head"),
            P("dp", "ctx", "head"),
            P("dp", "ctx", "head"),
            P("dp", "ctx", "head"),
            P(("ctx", "dp"), "head", None),
        ),
        check_vma=False,
    )
```

time: 555 us -> 104 us (0.19)
  the two profiles are of different devices: /device:TPU:1 before, /device:TPU:33 now
where the time goes in v1:
time: 104 us
  Pallas kernels  96.8 us (93%)
  local copies, waits for them, and re-layouts  6.03 us (6%)
    pallas_call x1, Pallas kernels, shards(): pl.pallas_call(kernel, out_shape=(jax.ShapeDtypeStruct((length, DOUT // 4...  96.8 us
    unnamed x11, local copies, waits for them, and re-layouts  6.03 us

profile of v1, /device:TPU:33, one launch (start us, length us, event | category | flops | bytes accessed | tf_op | source)
XLA Modules:
  0.0 103.5 jit_solution(2363613468757030140)
XLA Ops:
  0.6 96.8 %step.1 = (bf16[256,768]{1,0:T(8,128)(2,1)}, bf16[256,1024]{1,0:T(8,128)(2,1)}, bf16[256,1024]{1,0:T(8,128)(2,1)}, bf16[256,1024]{1,0:T(8,128)(2,1)}, f32[16,3072]{1,0:T(8,128)}) custom-call(bf16[256,1024]{1,0:T(8,128)(2,1)} %bitcast.12, bf16[256,1024]{1,0:T(8,128)(2,1)} %bitcast.13, bf16[256,1024]{1,0:T(8,128)(2,1)} %bitcast.14, f32[8,256]{1,0:T(8,128)} %bitcast.21, ...), custom_call_target="tpu_custom_call" | custom-call | tf_op jit(solution)/shard_map/step/pallas_call | solution.py:501
  97.5 0.0 copy-start.1
  97.5 0.0 copy-start
  97.5 1.9 %copy.16 = bf16[1,256,768]{2,1,0:T(8,128)(2,1)} copy(bf16[1,256,768]{2,1,0:T(8,128)(2,1)} %bitcast.18) | data formatting | bytes 786432
  99.3 0.0 copy-start.2
  99.3 1.9 %copy.17 = bf16[1,256,1024]{2,1,0:T(8,128)(2,1)} copy(bf16[1,256,1024]{2,1,0:T(8,128)(2,1)} %bitcast.17) | data formatting | bytes 1048576
  101.3 0.0 copy-done.1
  101.3 0.8 copy.18
  102.0 0.0 copy-done
  102.1 0.8 copy.19
  102.8 0.0 copy-done.2
  102.8 0.7 copy.20
Async XLA Ops:
  97.5 3.8 %copy-start.1 = (bf16[256,1024]{1,0:T(8,128)(2,1)S(1)}, bf16[256,1024]{1,0:T(8,128)(2,1)}, u32[]{:S(2)}) copy-start(bf16[256,1024]{1,0:T(8,128)(2,1)} %get-tuple-element.12) | copy-start | bytes 1572868
  97.5 4.6 %copy-start = (bf16[256,1024]{1,0:T(8,128)(2,1)S(1)}, bf16[256,1024]{1,0:T(8,128)(2,1)}, u32[]{:S(2)}) copy-start(bf16[256,1024]{1,0:T(8,128)(2,1)} %get-tuple-element.13) | copy-start | bytes 1572868
  99.3 3.5 %copy-start.2 = (f32[16,3072]{1,0:T(8,128)S(1)}, f32[16,3072]{1,0:T(8,128)}, u32[]{:S(2)}) copy-start(f32[16,3072]{1,0:T(8,128)} %get-tuple-element.14) | copy-start | bytes 589828

commit v2 on v1

v2 whole, which is shorter than its diff:
```python
import jax
import jax.numpy as jnp
from jax import lax
from jax.experimental import pallas as pl
from jax.experimental.pallas import tpu as pltpu
from jax.sharding import PartitionSpec as P

DH = 128
BLOCK = 256
HEADS = 8
DOUT = 3072
HALF = DOUT // 2
CHIPS = 16
SCALE = 1.0 / DH
F32 = jnp.float32
BF16 = jnp.bfloat16
NT = (((1,), (1,)), ((), ()))
NN = (((1,), (0,)), ((), ()))
TN = (((0,), (0,)), ((), ()))


def mm(a, b, dims):
    return lax.dot_general(a, b, dims, preferred_element_type=F32)


class Ids:
    def __init__(self):
        self.names = {}

    def __call__(self, *name):
        return self.names.setdefault(name, len(self.names))


def kernel(
    q_in, k_in, v_in, ld_in, w_in, go_in,
    mixed_out, qg_out, kg_out, vg_out, wg_out,
    q_ref, k_ref, v_ref, ld_ref, go_ref, mixed_ref, qg_ref, kg_ref, vg_ref, wg_ref,
    panel, pt, cum, ccol, probs, intra, kpart, vpart, att, attp, gh,
    cf, sf, tf, rf, ef, inf, lowf, low, cb, sb, tb, rb, eb, inb, lowb, back,
    go_sib, att_t, att_sib,
    wp, xb, yb, wacc, wa, xa, ya, xz,
    mp, macc, mr1, mr2,
    ssem, rsem, a2a_s, a2a_r, isem, osem,
):
    ctx, head, dp = lax.axis_index("ctx"), lax.axis_index("head"), lax.axis_index("dp")
    core, chip = ctx % 2, ctx // 2
    x, y = chip % 4, ctx // 8
    a = x * (1 - core) + y * core
    b = y * (1 - core) + x * core
    ap, am, ao = (a + 1) % 4, (a + 3) % 4, (a + 2) % 4
    bp, bm, bo = (b + 1) % 4, (b + 3) % 4, (b + 2) % 4
    z, zo = dp, 1 - dp

    def at(a1, b1):
        x1 = a1 * (1 - core) + b1 * core
        y1 = b1 * (1 - core) + a1 * core
        return ((y1 * 4 + x1) * 2 + core, head, dp)

    dev_ap, dev_am, dev_bp, dev_bm = at(ap, b), at(am, b), at(a, bp), at(a, bm)
    dev_sib = (ctx + 1 - 2 * core, head, dp)
    dev_z = (ctx, head, zo)
    h1 = head + 1 - 2 * (head % 2)
    h2 = (head + 2) % 4
    h3 = (h1 + 2) % 4
    dev_h1, dev_h2 = (ctx, h1, dp), (ctx, h2, dp)

    ids = Ids()
    started = []

    def xfer(name, src, dst, dev):
        i = ids(*name)
        return pltpu.make_async_remote_copy(
            src_ref=src, dst_ref=dst, send_sem=ssem.at[i], recv_sem=rsem.at[i],
            device_id=dev, device_id_type=pl.DeviceIdType.MESH,
        )

    def send(name, src, dst, dev):
        copy = xfer(name, src, dst, dev)
        copy.start()
        started.append(copy)

    def recv(name, ref, dev):
        xfer(name, ref, ref, dev).wait_recv()

    def slot(a1, b1, z1):
        return core * 32 + z1 * 16 + b1 * 4 + a1

    mine = slot(a, b, z)
    pairs = ((w_in, panel.at[mine]), (ld_in, ld_ref), (k_in, k_ref), (v_in, v_ref), (q_in, q_ref), (go_in, go_ref))
    loads = [pltpu.make_async_copy(src, dst, isem.at[i]) for i, (src, dst) in enumerate(pairs)]
    for load in loads:
        load.start()

    barrier = pltpu.get_barrier_semaphore()

    def greet(i, carry):
        pl.semaphore_signal(
            barrier, inc=1, device_id=((chip + i) % CHIPS * 2 + core, head, dp), device_id_type=pl.DeviceIdType.MESH
        )
        return carry

    lax.fori_loop(1, CHIPS, greet, 0)
    for dev in (dev_sib, dev_z, dev_h1, dev_h2):
        pl.semaphore_signal(barrier, inc=1, device_id=dev, device_id_type=pl.DeviceIdType.MESH)
    pl.semaphore_wait(barrier, CHIPS - 1 + 4)

    def whole(s):
        return panel.at[s]

    def part(s, h):
        return panel.at[s, :, pl.ds(h * HALF, HALF)]

    a_of = {0: a, 1: am, 2: ap, 3: ao}

    def b_sends(zi, k):
        zz = (z, zo)[zi]
        ref = whole(slot(a_of[k], b, zz))
        send(("bp", zi, k), ref, ref, dev_bp)
        send(("bm", zi, k), ref, ref, dev_bm)

    def a_sends(zi):
        ref = whole(slot(a, b, (z, zo)[zi]))
        send(("ap", zi), ref, ref, dev_ap)
        send(("am", zi), ref, ref, dev_am)

    def step_a(zi):
        zz = (z, zo)[zi]
        left, right = slot(am, b, zz), slot(ap, b, zz)
        recv(("ap", zi), whole(left), dev_am)
        send(("afp", zi), part(left, 0), part(left, 0), dev_ap)
        b_sends(zi, 1)
        recv(("am", zi), whole(right), dev_ap)
        send(("afm", zi), part(right, 1), part(right, 1), dev_am)
        b_sends(zi, 2)

    def step_ao(zi):
        far = slot(ao, b, (z, zo)[zi])
        recv(("afp", zi), part(far, 0), dev_am)
        recv(("afm", zi), part(far, 1), dev_ap)
        b_sends(zi, 3)
        sib_send(zi, 0)

    def step_b(zi, k):
        zz = (z, zo)[zi]
        below, above = slot(a_of[k], bm, zz), slot(a_of[k], bp, zz)
        recv(("bp", zi, k), whole(below), dev_bm)
        send(("bfp", zi, k), part(below, 0), part(below, 0), dev_bp)
        recv(("bm", zi, k), whole(above), dev_bp)
        send(("bfm", zi, k), part(above, 1), part(above, 1), dev_bm)

    def step_bo(zi, k):
        far = slot(a_of[k], bo, (z, zo)[zi])
        recv(("bfp", zi, k), part(far, 0), dev_bm)
        recv(("bfm", zi, k), part(far, 1), dev_bp)

    def step_z():
        recv(("z",), whole(slot(a, b, zo)), dev_z)
        a_sends(1)
        b_sends(1, 0)

    def row(c1, b1, z1):
        return panel.at[pl.ds(c1 * 32 + z1 * 16 + b1 * 4, 4)]

    def sib_send(zi, k):
        ref = row(core, (b, bm, bp, bo)[k], (z, zo)[zi])
        send(("sib", zi, k), ref, ref, dev_sib)

    def sib_recv(zi, k):
        recv(("sib", zi, k), row(1 - core, (a, am, ap, ao)[k], (z, zo)[zi]), dev_sib)

    loads[0].wait()
    send(("z",), whole(mine), whole(mine), dev_z)
    a_sends(0)
    b_sends(0, 0)
    for load in loads[1:4]:
        load.wait()

    t_row = lax.broadcasted_iota(jnp.int32, (BLOCK, BLOCK), 0)
    t_col = lax.broadcasted_iota(jnp.int32, (BLOCK, BLOCK), 1)
    upper = (t_row <= t_col).astype(F32)
    cum[...] = jnp.dot(ld_ref[...], upper, precision=lax.Precision.HIGHEST, preferred_element_type=F32)

    def lanes(h):
        return pl.ds(pl.multiple_of(h * DH, DH), DH)

    def weights(h):
        col = ccol[h]
        spread = jnp.concatenate([col, col], axis=1) - cum[pl.ds(h, 1), :]
        rows = lax.broadcasted_iota(jnp.int32, (BLOCK, BLOCK), 0)
        cols = lax.broadcasted_iota(jnp.int32, (BLOCK, BLOCK), 1)
        return jnp.exp(jnp.where(rows >= cols, spread, -jnp.inf))

    def pieces(buf, h, total, decay):
        for r in range(4):
            buf[h * 4 + r, 0:32, :] = total[r * 32 : (r + 1) * 32]
            buf[h * 4 + r, 32:40, :] = jnp.broadcast_to(decay, (8, DH))

    def fwd_share(h, carry):
        wide = jnp.broadcast_to(cum[pl.ds(h, 1), :], (DH, BLOCK))
        col = wide.T
        ccol[h] = col
        last = col[BLOCK - 1 : BLOCK, :]
        kw = (k_ref[:, lanes(h)].astype(F32) * jnp.exp(last - col)).astype(BF16)
        pieces(cf, h, mm(kw, v_ref[:, lanes(h)], TN), jnp.exp(last))
        return carry

    def halves(own, sib, j, first):
        p, o = own[core * CHIPS + j], sib[j]
        return jnp.where(core == first, p, o), jnp.where(core == first, o, p)

    def own_half(buf):
        return buf.at[pl.ds(core * CHIPS, CHIPS)]

    def other_half(buf):
        return buf.at[pl.ds((1 - core) * CHIPS, CHIPS)]

    def merge(own, sib, out, first):
        def go(j, carry):
            p, s = halves(own, sib, j, first)
            out[j, 0:32, :] = s[32:33] * p[0:32] + s[0:32]
            out[j, 32:40, :] = s[32:40] * p[32:40]
            return carry

        lax.fori_loop(0, CHIPS, go, 0)

    def split(own, sib, got, out, out_sib, first):
        def go(j, carry):
            p, _ = halves(own, sib, j, first)
            early = got[j].astype(F32)
            late = p[32:33] * early + p[0:32]
            out[core * CHIPS + j] = jnp.where(core == first, early, late).astype(BF16)
            out_sib[j] = jnp.where(core == first, late, early).astype(BF16)
            return carry

        lax.fori_loop(0, CHIPS, go, 0)

    def a2a(n, src, dst, i, out):
        other = (chip + i) % CHIPS if out else (chip + CHIPS - i) % CHIPS
        return pltpu.make_async_remote_copy(
            src_ref=src.at[other], dst_ref=dst.at[chip if out else other],
            send_sem=a2a_s.at[n, i], recv_sem=a2a_r.at[n, i],
            device_id=(other * 2 + core, head, dp), device_id_type=pl.DeviceIdType.MESH,
        )

    def a2a_start(n, src, dst):
        def go(i, carry):
            a2a(n, src, dst, i, True).start()
            return carry

        lax.fori_loop(1, CHIPS, go, 0)
        dst[chip] = src[chip]

    def a2a_recv(n, src, dst):
        def go(i, carry):
            a2a(n, src, dst, i, False).wait_recv()
            return carry

        lax.fori_loop(1, CHIPS, go, 0)

    def a2a_sent(n, src, dst):
        def go(i, carry):
            a2a(n, src, dst, i, True).wait_send()
            return carry

        lax.fori_loop(1, CHIPS, go, 0)

    def scan(got, out, reverse):
        def go(i, state):
            at_chip = CHIPS - 1 - i if reverse else i
            out[at_chip] = state.astype(BF16)
            return state * got[at_chip, 32:33, :] + got[at_chip, 0:32, :]

        lax.fori_loop(0, CHIPS, go, jnp.zeros((32, DH), F32))

    def state_of(buf, h):
        return buf[pl.ds(h * 4, 4)].reshape(DH, DH)

    lax.fori_loop(0, HEADS, fwd_share, 0)
    send(("f", 0), other_half(cf), sf, dev_sib)
    step_a(0)
    recv(("f", 0), sf, dev_sib)
    merge(cf, sf, tf, 0)
    a2a_start(0, tf, rf)
    loads[4].wait()
    loads[5].wait()
    send(("go",), go_ref, go_sib, dev_sib)

    def inside(h, carry):
        scores = mm(q_ref[:, lanes(h)], k_ref[:, lanes(h)], NT)
        p = (scores * SCALE * weights(h)).astype(BF16)
        probs[h] = p
        intra[:, lanes(h)] = mm(p, v_ref[:, lanes(h)], NN)
        return carry

    lax.fori_loop(0, 2, inside, 0)
    step_ao(0)
    step_z()
    step_b(0, 0)
    lax.fori_loop(2, 5, inside, 0)
    step_b(0, 1)
    step_b(0, 2)
    a2a_recv(0, tf, rf)
    scan(rf, ef, False)
    a2a_start(1, ef, inf)
    step_a(1)
    lax.fori_loop(5, HEADS, inside, 0)
    step_b(0, 3)
    sib_send(0, 1)
    sib_send(0, 2)
    step_ao(1)
    step_b(1, 0)

    a2a_recv(1, ef, inf)
    split(cf, sf, inf, low, lowf, 0)
    send(("f", 1), lowf, own_half(low), dev_sib)

    r = lax.broadcasted_iota(jnp.int32, (1024, DH), 0)
    place = r >> 4
    pc, pz, pb, pa = place >> 5, (place >> 4) & 1, (place >> 2) & 3, place & 3
    px = jnp.where(pc == 0, pa, pb)
    py = jnp.where(pc == 0, pb, pa)
    feature = 2 * ((((py * 4) + px) * 2 + pc) * 2 + pz) + ((r >> 3) & 1)
    lane = lax.broadcasted_iota(jnp.int32, (1024, DH), 1)
    same = feature == lane
    for h in range(HEADS):
        pt[:, h * DH : (h + 1) * DH] = jnp.where(same & ((r & 7) == h), 1.0, 0.0).astype(BF16)

    step_b(1, 1)
    step_b(1, 2)
    recv(("f", 1), other_half(low), dev_sib)

    def attend(h, carry):
        inter = mm(q_ref[:, lanes(h)], state_of(low, h), NN)
        factor = SCALE * jnp.exp(ccol[h])
        att[:, lanes(h)] = (intra[:, lanes(h)] + inter * factor).astype(BF16)
        return carry

    lax.fori_loop(0, HEADS, attend, 0)
    step_b(1, 3)
    sib_send(1, 1)
    sib_send(1, 2)

    def turn(i, carry):
        rows = pl.ds(pl.multiple_of(i * 256, 256), 256)
        att_t[rows, :] = mm(pt[rows, :], att[...], NT).astype(BF16)
        attp[:, rows] = mm(att[...], pt[rows, :], NT).astype(BF16)
        return carry

    lax.fori_loop(0, 4, turn, 0)
    other_rows = pl.ds(pl.multiple_of((1 - core) * 512, 512), 512)
    send(("att",), att_t.at[other_rows], att_sib, dev_sib)
    for k in range(4):
        step_bo(0, k)
    sib_send(0, 3)

    recv(("go",), go_sib, dev_sib)
    recv(("att",), att_sib, dev_sib)
    lo, hi = pl.ds(0, HALF), pl.ds(HALF, HALF)

    def widen(ref):
        return ref.astype(F32)

    def rows_b(b1):
        return pl.ds(pl.multiple_of(b1 * 64, 64), 64)

    def rows_a(a1):
        return pl.ds(pl.multiple_of(a1 * 16, 16), 16)

    def w_block(zi):
        zz = (zo, z)[zi]
        own = pl.ds(pl.multiple_of(core * 512 + zz * 256, 256), 256)
        sib = pl.ds(pl.multiple_of(zz * 256, 256), 256)

        def go(n, carry):
            cols = pl.ds(pl.multiple_of(n * 256, 256), 256)
            value = mm(att_t[own, :], go_ref[:, cols], NN) + mm(att_sib[sib, :], go_sib[:, cols], NN)
            wp[zi, :, cols] = value.astype(BF16)
            return carry

        lax.fori_loop(0, 12, go, 0)

    def w_first(zi):
        w_block(zi)
        send(("w", zi, 0), wp.at[zi, rows_b(bo), lo], xb.at[zi, 0], dev_bp)
        send(("w", zi, 1), wp.at[zi, rows_b(bo), hi], xb.at[zi, 1], dev_bm)
        send(("w", zi, 2), wp.at[zi, rows_b(bp), hi], yb.at[zi, 0, :, hi], dev_bp)
        send(("w", zi, 3), wp.at[zi, rows_b(bm), lo], yb.at[zi, 1, :, lo], dev_bm)

    def w_relay(zi):
        recv(("w", zi, 0), xb.at[zi, 0], dev_bm)
        wp[zi, rows_b(bp), lo] = (widen(wp[zi, rows_b(bp), lo]) + widen(xb[zi, 0])).astype(BF16)
        send(("w", zi, 4), wp.at[zi, rows_b(bp), lo], yb.at[zi, 0, :, lo], dev_bp)
        recv(("w", zi, 1), xb.at[zi, 1], dev_bp)
        wp[zi, rows_b(bm), hi] = (widen(wp[zi, rows_b(bm), hi]) + widen(xb[zi, 1])).astype(BF16)
        send(("w", zi, 5), wp.at[zi, rows_b(bm), hi], yb.at[zi, 1, :, hi], dev_bm)

    def v_first(zi):
        recv(("w", zi, 2), yb.at[zi, 0, :, hi], dev_bm)
        recv(("w", zi, 3), yb.at[zi, 1, :, lo], dev_bp)
        recv(("w", zi, 4), yb.at[zi, 0, :, lo], dev_bm)
        recv(("w", zi, 5), yb.at[zi, 1, :, hi], dev_bp)

        def go(n, carry):
            cols = pl.ds(pl.multiple_of(n * 256, 256), 256)
            total = widen(wp[zi, rows_b(b), cols]) + widen(yb[zi, 0, :, cols]) + widen(yb[zi, 1, :, cols])
            wacc[zi, :, cols] = total
            wa[zi, :, cols] = total.astype(BF16)
            return carry

        lax.fori_loop(0, 12, go, 0)
        send(("v", zi, 0), wa.at[zi, rows_a(ao), lo], xa.at[zi, 0], dev_ap)
        send(("v", zi, 1), wa.at[zi, rows_a(ao), hi], xa.at[zi, 1], dev_am)
        send(("v", zi, 2), wa.at[zi, rows_a(ap), hi], ya.at[zi, 0, :, hi], dev_ap)
        send(("v", zi, 3), wa.at[zi, rows_a(am), lo], ya.at[zi, 1, :, lo], dev_am)

    def v_relay(zi):
        recv(("v", zi, 0), xa.at[zi, 0], dev_am)
        wa[zi, rows_a(ap), lo] = (widen(wa[zi, rows_a(ap), lo]) + widen(xa[zi, 0])).astype(BF16)
        send(("v", zi, 4), wa.at[zi, rows_a(ap), lo], ya.at[zi, 0, :, lo], dev_ap)
        recv(("v", zi, 1), xa.at[zi, 1], dev_ap)
        wa[zi, rows_a(am), hi] = (widen(wa[zi, rows_a(am), hi]) + widen(xa[zi, 1])).astype(BF16)
        send(("v", zi, 5), wa.at[zi, rows_a(am), hi], ya.at[zi, 1, :, hi], dev_am)

    def v_last(zi):
        recv(("v", zi, 2), ya.at[zi, 0, :, hi], dev_am)
        recv(("v", zi, 3), ya.at[zi, 1, :, lo], dev_ap)
        recv(("v", zi, 4), ya.at[zi, 0, :, lo], dev_am)
        recv(("v", zi, 5), ya.at[zi, 1, :, hi], dev_ap)
        return wacc[zi, rows_a(a), :] + widen(ya[zi, 0]) + widen(ya[zi, 1])

    w_first(0)
    w_first(1)

    for k in range(4):
        step_bo(1, k)
    sib_send(1, 3)
    for zi in range(2):
        for k in range(4):
            sib_recv(zi, k)

    def mix(dest, store):
        def go(n, carry):
            cols = pl.ds(pl.multiple_of(dest * 768 + n * 256, 256), 256)
            w = panel[:, :, cols].reshape(1024, 256)
            store(pl.ds(pl.multiple_of(n * 256, 256), 256), mm(attp[...], w, NN))
            return carry

        lax.fori_loop(0, 3, go, 0)

    def store_at(dest):
        def store(cols, value):
            mp[dest, :, cols] = value.astype(BF16)

        return store

    def store_own(cols, value):
        macc[:, cols] = value

    mix(h3, store_at(h3))
    send(("m", 0), mp.at[h3], mr1.at[0], dev_h1)
    mix(h1, store_at(h1))
    send(("m", 1), mp.at[h1], mr1.at[1], dev_h1)

    def heads_grad(i, carry):
        rows = panel[pl.ds(i * 16, 16)].reshape(256, DOUT)
        cols = pl.ds(pl.multiple_of(i * 256, 256), 256)
        gh[:, cols] = mm(go_ref[...], rows, NT).astype(BF16)
        return carry

    lax.fori_loop(0, 4, heads_grad, 0)
    by_head = []
    for n in range(4):
        by_head.append(mm(gh[...], pt[:, n * 256 : (n + 1) * 256], NN).astype(BF16))
    for n in range(4):
        gh[:, n * 256 : (n + 1) * 256] = by_head[n]

    def bwd_share(h, carry):
        qw = (q_ref[:, lanes(h)].astype(F32) * (SCALE * jnp.exp(ccol[h]))).astype(BF16)
        last = ccol[h, BLOCK - 1 : BLOCK, :]
        pieces(cb, h, mm(qw, gh[:, lanes(h)], TN), jnp.exp(last))
        return carry

    lax.fori_loop(0, HEADS, bwd_share, 0)
    send(("k", 0), other_half(cb), sb, dev_sib)
    w_relay(0)
    recv(("k", 0), sb, dev_sib)
    merge(cb, sb, tb, 1)
    a2a_start(2, tb, rb)
    w_relay(1)
    mix(h2, store_at(h2))

    def grads(h, carry):
        g, kk, vv, qq = gh[:, lanes(h)], k_ref[:, lanes(h)], v_ref[:, lanes(h)], q_ref[:, lanes(h)]
        dp_h = (mm(g, vv, NT) * SCALE * weights(h)).astype(BF16)
        factor = SCALE * jnp.exp(ccol[h])
        qg = mm(dp_h, kk, NN) + mm(g, state_of(low, h), NT) * factor
        qg_ref[:, lanes(h)] = qg.astype(BF16)
        kpart[:, lanes(h)] = mm(dp_h, qq, TN)
        vpart[:, lanes(h)] = mm(probs[h], g, TN)
        return carry

    lax.fori_loop(0, 2, grads, 0)
    v_first(0)
    recv(("m", 0), mr1.at[0], dev_h1)
    mp[h2] = (widen(mp[h2]) + widen(mr1[0])).astype(BF16)
    send(("m", 2), mp.at[h2], mr2, dev_h2)
    a2a_recv(2, tb, rb)
    scan(rb, eb, True)
    a2a_start(3, eb, inb)
    lax.fori_loop(2, 5, grads, 0)
    v_relay(0)
    v_first(1)
    lax.fori_loop(5, HEADS, grads, 0)
    wa[0, rows_a(a), :] = v_last(0).astype(BF16)
    send(("vz",), wa.at[0, rows_a(a)], xz, dev_z)
    v_relay(1)

    a2a_recv(3, eb, inb)
    split(cb, sb, inb, back, lowb, 1)
    send(("k", 1), lowb, own_half(back), dev_sib)
    outs = [
        pltpu.make_async_copy(src, dst, osem.at[i])
        for i, (src, dst) in enumerate(
            ((qg_ref, qg_out), (kg_ref, kg_out), (vg_ref, vg_out), (mixed_ref, mixed_out), (wg_ref, wg_out))
        )
    ]
    outs[0].start()
    mix(head, store_own)
    recv(("k", 1), other_half(back), dev_sib)

    def finish(h, carry):
        col = ccol[h]
        tail = jnp.exp(col[BLOCK - 1 : BLOCK, :] - col)
        state = state_of(back, h)
        kg = kpart[:, lanes(h)] + tail * mm(v_ref[:, lanes(h)], state, NT)
        vg = vpart[:, lanes(h)] + tail * mm(k_ref[:, lanes(h)], state, NN)
        kg_ref[:, lanes(h)] = kg.astype(BF16)
        vg_ref[:, lanes(h)] = vg.astype(BF16)
        return carry

    lax.fori_loop(0, HEADS, finish, 0)
    outs[1].start()
    outs[2].start()

    wg_ref[...] = v_last(1)
    recv(("vz",), xz, dev_z)
    wg_ref[...] += widen(xz[...])
    outs[4].start()

    recv(("m", 1), mr1.at[1], dev_h1)
    recv(("m", 2), mr2, dev_h2)
    mixed_ref[...] = (macc[...] + widen(mr1[1]) + widen(mr2[...])).astype(BF16)
    outs[3].start()

    for copy in started:
        copy.wait_send()
    for n, src, dst in ((0, tf, rf), (1, ef, inf), (2, tb, rb), (3, eb, inb)):
        a2a_sent(n, src, dst)
    for out in outs:
        out.wait()


def hand_out(*refs):
    n = len(refs) // 3
    given, out, held, sems = refs[:n], refs[n : 2 * n], refs[2 * n : 3 * n], refs[-1]
    first = [pltpu.make_async_copy(given[i], held[i], sems.at[0, i]) for i in range(n)]
    second = [pltpu.make_async_copy(held[i], out[i], sems.at[1, i]) for i in range(n)]
    for copy in first:
        copy.start()
    for i in range(n):
        first[i].wait()
        second[i].start()
    for copy in second:
        copy.wait()


def shards(queries, keys, values, log_decay, w_out, grad_out):
    hbm = pl.BlockSpec(memory_space=pl.ANY)
    length = queries.shape[1]
    features = HEADS * DH
    shapes = (
        jax.ShapeDtypeStruct((length, DOUT // 4), BF16),
        jax.ShapeDtypeStruct((length, features), BF16),
        jax.ShapeDtypeStruct((length, features), BF16),
        jax.ShapeDtypeStruct((length, features), BF16),
        jax.ShapeDtypeStruct((16, DOUT), F32),
    )
    whole = pltpu.VMEM((length, features), BF16)
    wide = pltpu.VMEM((length, features), F32)
    piece = pltpu.VMEM((CHIPS, 40, DH), F32)
    state = pltpu.VMEM((CHIPS, 32, DH), BF16)
    scan = [
        pltpu.VMEM((2 * CHIPS, 40, DH), F32), piece, piece, piece,
        state, state, state, pltpu.VMEM((2 * CHIPS, 32, DH), BF16),
    ]

    results = pl.pallas_call(
        kernel,
        out_shape=shapes,
        in_specs=[hbm] * 6,
        out_specs=(hbm,) * 5,
        scratch_shapes=[
            whole,
            whole,
            whole,
            pltpu.VMEM((HEADS, BLOCK), F32),
            pltpu.VMEM((BLOCK, DOUT), BF16),
            pltpu.VMEM((BLOCK, DOUT // 4), BF16),
            whole,
            whole,
            whole,
            pltpu.VMEM((16, DOUT), F32),
            pltpu.VMEM((64, 16, DOUT), BF16),
            pltpu.VMEM((features, features), BF16),
            pltpu.VMEM((HEADS, BLOCK), F32),
            pltpu.VMEM((HEADS, BLOCK, DH), F32),
            pltpu.VMEM((HEADS, BLOCK, BLOCK), BF16),
            wide,
            wide,
            wide,
            whole,
            whole,
            whole,
            *scan,
            *scan,
            pltpu.VMEM((BLOCK, DOUT), BF16),
            pltpu.VMEM((features, BLOCK), BF16),
            pltpu.VMEM((512, BLOCK), BF16),
            pltpu.VMEM((2, 256, DOUT), BF16),
            pltpu.VMEM((2, 2, 64, HALF), BF16),
            pltpu.VMEM((2, 2, 64, DOUT), BF16),
            pltpu.VMEM((2, 64, DOUT), F32),
            pltpu.VMEM((2, 64, DOUT), BF16),
            pltpu.VMEM((2, 2, 16, HALF), BF16),
            pltpu.VMEM((2, 2, 16, DOUT), BF16),
            pltpu.VMEM((16, DOUT), BF16),
            pltpu.VMEM((4, BLOCK, 768), BF16),
            pltpu.VMEM((BLOCK, 768), F32),
            pltpu.VMEM((2, BLOCK, 768), BF16),
            pltpu.VMEM((BLOCK, 768), BF16),
            pltpu.SemaphoreType.DMA((88,)),
            pltpu.SemaphoreType.DMA((88,)),
            pltpu.SemaphoreType.DMA((4, CHIPS)),
            pltpu.SemaphoreType.DMA((4, CHIPS)),
            pltpu.SemaphoreType.DMA((6,)),
            pltpu.SemaphoreType.DMA((5,)),
        ],
        compiler_params=pltpu.CompilerParams(
            collective_id=0, has_side_effects=True, vmem_limit_bytes=60 * 1024 * 1024
        ),
        name="step",
    )(queries[0], keys[0], values[0], log_decay[0], w_out.reshape(16, DOUT), grad_out[0])
    mixed, qg, kg, vg, wg = pl.pallas_call(
        hand_out,
        out_shape=shapes,
        in_specs=[hbm] * 5,
        out_specs=(hbm,) * 5,
        scratch_shapes=[*(pltpu.VMEM(s.shape, s.dtype) for s in shapes), pltpu.SemaphoreType.DMA((2, 5))],
        compiler_params=pltpu.CompilerParams(vmem_limit_bytes=60 * 1024 * 1024),
        name="hand_out",
    )(*results)
    return mixed[None], qg[None], kg[None], vg[None], wg.reshape(2, HEADS, DOUT)


def solution(mesh):
    return jax.shard_map(
        shards,
        mesh=mesh,
        in_specs=(
            P("dp", "ctx", "head"),
            P("dp", "ctx", "head"),
            P("dp", "ctx", "head"),
            P("dp", "head", "ctx"),
            P(("ctx", "dp"), "head", None),
            P("dp", "ctx", None),
        ),
        out_specs=(
            P("dp", "ctx", "head"),
            P("dp", "ctx", "head"),
            P("dp", "ctx", "head"),
            P("dp", "ctx", "head"),
            P(("ctx", "dp"), "head", None),
        ),
        check_vma=False,
    )
```

time: 104 us -> 86.5 us (0.83)
  the two profiles are of different devices: /device:TPU:33 before, /device:TPU:2 now
where the time goes in v2:
time: 86.5 us; the launch traced here: 86.4 us
  Pallas kernels  85.8 us (99%)
    pallas_call x1, Pallas kernels, shards(): pl.pallas_call(kernel, out_shape=shapes, in_specs=[hbm] * 6, out_specs=(h...  83.3 us
    pallas_call x1, Pallas kernels, shards(): pl.pallas_call(hand_out, out_shape=shapes, in_specs=[hbm] * 5, out_specs=...  2.44 us

profile of v2, /device:TPU:2, one launch (start us, length us, event | category | flops | bytes accessed | tf_op | source)
XLA Modules:
  0.0 86.4 jit_solution(9242299580190359687)
XLA Ops:
  0.6 83.3 %step.1 = (bf16[256,768]{1,0:T(8,128)(2,1)}, bf16[256,1024]{1,0:T(8,128)(2,1)}, bf16[256,1024]{1,0:T(8,128)(2,1)}, bf16[256,1024]{1,0:T(8,128)(2,1)}, f32[16,3072]{1,0:T(8,128)}) custom-call(bf16[256,1024]{1,0:T(8,128)(2,1)} %bitcast.12, bf16[256,1024]{1,0:T(8,128)(2,1)} %bitcast.13, bf16[256,1024]{1,0:T(8,128)(2,1)} %bitcast.14, f32[8,256]{1,0:T(8,128)} %bitcast.16, ...), custom_call_target="tpu_custom_call" | custom-call | tf_op jit(solution)/shard_map/step/pallas_call | solution.py:597
  84.0 2.4 %hand_out.1 = (bf16[256,768]{1,0:T(8,128)(2,1)}, bf16[256,1024]{1,0:T(8,128)(2,1)}, bf16[256,1024]{1,0:T(8,128)(2,1)}, bf16[256,1024]{1,0:T(8,128)(2,1)}, f32[16,3072]{1,0:T(8,128)}) custom-call(bf16[256,768]{1,0:T(8,128)(2,1)} %get-tuple-element.15.refs_0_, bf16[256,1024]{1,0:T(8,128)(2,1)} %get-tuple-element.16.refs_1_, ...), custom_call_target="tpu_custom_call" | custom-call | tf_op jit(solution)/shard_map/hand_out/pallas_call | solution.py:653

commit v3 on v2

--- a/solution.py
+++ b/solution.py
@@ -38,7 +38,7 @@
     panel, pt, cum, ccol, probs, intra, kpart, vpart, att, attp, gh,
     cf, sf, tf, rf, ef, inf, lowf, low, cb, sb, tb, rb, eb, inb, lowb, back,
     go_sib, att_t, att_sib,
-    wp, xb, yb, wacc, wa, xa, ya, xz,
+    wp, xb, yb, wacc, wa, ya, xz,
     mp, macc, mr1, mr2,
     ssem, rsem, a2a_s, a2a_r, isem, osem,
 ):
@@ -56,7 +56,7 @@
         y1 = b1 * (1 - core) + a1 * core
         return ((y1 * 4 + x1) * 2 + core, head, dp)
 
-    dev_ap, dev_am, dev_bp, dev_bm = at(ap, b), at(am, b), at(a, bp), at(a, bm)
+    dev_ap, dev_am, dev_ao, dev_bp, dev_bm = at(ap, b), at(am, b), at(ao, b), at(a, bp), at(a, bm)
     dev_sib = (ctx + 1 - 2 * core, head, dp)
     dev_z = (ctx, head, zo)
     h1 = head + 1 - 2 * (head % 2)
@@ -102,6 +102,35 @@
     lax.fori_loop(1, CHIPS, greet, 0)
     for dev in (dev_sib, dev_z, dev_h1, dev_h2):
         pl.semaphore_signal(barrier, inc=1, device_id=dev, device_id_type=pl.DeviceIdType.MESH)
+    for load in loads[1:4]:
+        load.wait()
+
+    t_row = lax.broadcasted_iota(jnp.int32, (BLOCK, BLOCK), 0)
+    t_col = lax.broadcasted_iota(jnp.int32, (BLOCK, BLOCK), 1)
+    upper = (t_row <= t_col).astype(F32)
+    cum[...] = jnp.dot(ld_ref[...], upper, precision=lax.Precision.HIGHEST, preferred_element_type=F32)
+
+    def heads(first, last, body):
+        lax.fori_loop(first, last, body, 0, unroll=2 if (last - first) % 2 == 0 else 1)
+
+    def lanes(h):
+        return pl.ds(pl.multiple_of(h * DH, DH), DH)
+
+    def pieces(buf, h, total, decay):
+        for r in range(4):
+            buf[h * 4 + r, 0:32, :] = total[r * 32 : (r + 1) * 32]
+            buf[h * 4 + r, 32:40, :] = jnp.broadcast_to(decay, (8, DH))
+
+    def fwd_share(h, carry):
+        wide = jnp.broadcast_to(cum[pl.ds(h, 1), :], (DH, BLOCK))
+        col = wide.T
+        ccol[h] = col
+        last = col[BLOCK - 1 : BLOCK, :]
+        kw = (k_ref[:, lanes(h)].astype(F32) * jnp.exp(last - col)).astype(BF16)
+        pieces(cf, h, mm(kw, v_ref[:, lanes(h)], TN), jnp.exp(last))
+        return carry
+
+    heads(0, 4, fwd_share)
     pl.semaphore_wait(barrier, CHIPS - 1 + 4)
 
     def whole(s):
@@ -122,21 +151,19 @@
         ref = whole(slot(a, b, (z, zo)[zi]))
         send(("ap", zi), ref, ref, dev_ap)
         send(("am", zi), ref, ref, dev_am)
+        send(("ao", zi), ref, ref, dev_ao)
 
     def step_a(zi):
         zz = (z, zo)[zi]
         left, right = slot(am, b, zz), slot(ap, b, zz)
         recv(("ap", zi), whole(left), dev_am)
-        send(("afp", zi), part(left, 0), part(left, 0), dev_ap)
         b_sends(zi, 1)
         recv(("am", zi), whole(right), dev_ap)
-        send(("afm", zi), part(right, 1), part(right, 1), dev_am)
         b_sends(zi, 2)
 
     def step_ao(zi):
         far = slot(ao, b, (z, zo)[zi])
-        recv(("afp", zi), part(far, 0), dev_am)
-        recv(("afm", zi), part(far, 1), dev_ap)
+        recv(("ao", zi), whole(far), dev_ao)
         b_sends(zi, 3)
         sib_send(zi, 0)
 
@@ -172,17 +199,6 @@
     send(("z",), whole(mine), whole(mine), dev_z)
     a_sends(0)
     b_sends(0, 0)
-    for load in loads[1:4]:
-        load.wait()
-
-    t_row = lax.broadcasted_iota(jnp.int32, (BLOCK, BLOCK), 0)
-    t_col = lax.broadcasted_iota(jnp.int32, (BLOCK, BLOCK), 1)
-    upper = (t_row <= t_col).astype(F32)
-    cum[...] = jnp.dot(ld_ref[...], upper, precision=lax.Precision.HIGHEST, preferred_element_type=F32)
-
-    def lanes(h):
-        return pl.ds(pl.multiple_of(h * DH, DH), DH)
-
     def weights(h):
         col = ccol[h]
         spread = jnp.concatenate([col, col], axis=1) - cum[pl.ds(h, 1), :]
@@ -190,20 +206,6 @@
         cols = lax.broadcasted_iota(jnp.int32, (BLOCK, BLOCK), 1)
         return jnp.exp(jnp.where(rows >= cols, spread, -jnp.inf))
 
-    def pieces(buf, h, total, decay):
-        for r in range(4):
-            buf[h * 4 + r, 0:32, :] = total[r * 32 : (r + 1) * 32]
-            buf[h * 4 + r, 32:40, :] = jnp.broadcast_to(decay, (8, DH))
-
-    def fwd_share(h, carry):
-        wide = jnp.broadcast_to(cum[pl.ds(h, 1), :], (DH, BLOCK))
-        col = wide.T
-        ccol[h] = col
-        last = col[BLOCK - 1 : BLOCK, :]
-        kw = (k_ref[:, lanes(h)].astype(F32) * jnp.exp(last - col)).astype(BF16)
-        pieces(cf, h, mm(kw, v_ref[:, lanes(h)], TN), jnp.exp(last))
-        return carry
-
     def halves(own, sib, j, first):
         p, o = own[core * CHIPS + j], sib[j]
         return jnp.where(core == first, p, o), jnp.where(core == first, o, p)
@@ -217,8 +219,14 @@
     def merge(own, sib, out, first):
         def go(j, carry):
             p, s = halves(own, sib, j, first)
-            out[j, 0:32, :] = s[32:33] * p[0:32] + s[0:32]
-            out[j, 32:40, :] = s[32:40] * p[32:40]
+            out[j, 0:32, :] = (s[32:33] * p[0:32] + s[0:32]).astype(BF16)
+            decay = s[32:40] * p[32:40]
+            decay = jnp.concatenate([decay, decay], axis=0)
+            top = decay.astype(BF16).astype(F32)
+            mid = (decay - top).astype(BF16).astype(F32)
+            place = lax.broadcasted_iota(jnp.int32, (16, DH), 0)
+            three = jnp.where(place < 5, top, jnp.where(place < 10, mid, decay - top - mid))
+            out[j, 32:48, :] = three.astype(BF16)
             return carry
 
         lax.fori_loop(0, CHIPS, go, 0)
@@ -268,14 +276,16 @@
         def go(i, state):
             at_chip = CHIPS - 1 - i if reverse else i
             out[at_chip] = state.astype(BF16)
-            return state * got[at_chip, 32:33, :] + got[at_chip, 0:32, :]
+            three = got[at_chip, 32:48, :].astype(F32)
+            decay = three[0:1] + three[5:6] + three[10:11]
+            return state * decay + got[at_chip, 0:32, :].astype(F32)
 
         lax.fori_loop(0, CHIPS, go, jnp.zeros((32, DH), F32))
 
     def state_of(buf, h):
         return buf[pl.ds(h * 4, 4)].reshape(DH, DH)
 
-    lax.fori_loop(0, HEADS, fwd_share, 0)
+    heads(4, HEADS, fwd_share)
     send(("f", 0), other_half(cf), sf, dev_sib)
     step_a(0)
     recv(("f", 0), sf, dev_sib)
@@ -292,18 +302,18 @@
         intra[:, lanes(h)] = mm(p, v_ref[:, lanes(h)], NN)
         return carry
 
-    lax.fori_loop(0, 2, inside, 0)
+    heads(0, 2, inside)
     step_ao(0)
     step_z()
     step_b(0, 0)
-    lax.fori_loop(2, 5, inside, 0)
+    heads(2, 4, inside)
     step_b(0, 1)
     step_b(0, 2)
     a2a_recv(0, tf, rf)
     scan(rf, ef, False)
     a2a_start(1, ef, inf)
     step_a(1)
-    lax.fori_loop(5, HEADS, inside, 0)
+    heads(4, HEADS, inside)
     step_b(0, 3)
     sib_send(0, 1)
     sib_send(0, 2)
@@ -335,7 +345,7 @@
         att[:, lanes(h)] = (intra[:, lanes(h)] + inter * factor).astype(BF16)
         return carry
 
-    lax.fori_loop(0, HEADS, attend, 0)
+    heads(0, HEADS, attend)
     step_b(1, 3)
     sib_send(1, 1)
     sib_send(1, 2)
@@ -408,25 +418,13 @@
             return carry
 
         lax.fori_loop(0, 12, go, 0)
-        send(("v", zi, 0), wa.at[zi, rows_a(ao), lo], xa.at[zi, 0], dev_ap)
-        send(("v", zi, 1), wa.at[zi, rows_a(ao), hi], xa.at[zi, 1], dev_am)
-        send(("v", zi, 2), wa.at[zi, rows_a(ap), hi], ya.at[zi, 0, :, hi], dev_ap)
-        send(("v", zi, 3), wa.at[zi, rows_a(am), lo], ya.at[zi, 1, :, lo], dev_am)
-
-    def v_relay(zi):
-        recv(("v", zi, 0), xa.at[zi, 0], dev_am)
-        wa[zi, rows_a(ap), lo] = (widen(wa[zi, rows_a(ap), lo]) + widen(xa[zi, 0])).astype(BF16)
-        send(("v", zi, 4), wa.at[zi, rows_a(ap), lo], ya.at[zi, 0, :, lo], dev_ap)
-        recv(("v", zi, 1), xa.at[zi, 1], dev_ap)
-        wa[zi, rows_a(am), hi] = (widen(wa[zi, rows_a(am), hi]) + widen(xa[zi, 1])).astype(BF16)
-        send(("v", zi, 5), wa.at[zi, rows_a(am), hi], ya.at[zi, 1, :, hi], dev_am)
+        for n, (a1, dev) in enumerate(((ao, dev_ao), (ap, dev_ap), (am, dev_am))):
+            send(("v", zi, n), wa.at[zi, rows_a(a1)], ya.at[zi, n], dev)
 
     def v_last(zi):
-        recv(("v", zi, 2), ya.at[zi, 0, :, hi], dev_am)
-        recv(("v", zi, 3), ya.at[zi, 1, :, lo], dev_ap)
-        recv(("v", zi, 4), ya.at[zi, 0, :, lo], dev_am)
-        recv(("v", zi, 5), ya.at[zi, 1, :, hi], dev_ap)
-        return wacc[zi, rows_a(a), :] + widen(ya[zi, 0]) + widen(ya[zi, 1])
+        for n, dev in enumerate((dev_ao, dev_am, dev_ap)):
+            recv(("v", zi, n), ya.at[zi, n], dev)
+        return wacc[zi, rows_a(a), :] + widen(ya[zi, 0]) + widen(ya[zi, 1]) + widen(ya[zi, 2])
 
     w_first(0)
     w_first(1)
@@ -480,7 +478,7 @@
         pieces(cb, h, mm(qw, gh[:, lanes(h)], TN), jnp.exp(last))
         return carry
 
-    lax.fori_loop(0, HEADS, bwd_share, 0)
+    heads(0, HEADS, bwd_share)
     send(("k", 0), other_half(cb), sb, dev_sib)
     w_relay(0)
     recv(("k", 0), sb, dev_sib)
@@ -499,7 +497,7 @@
         vpart[:, lanes(h)] = mm(probs[h], g, TN)
         return carry
 
-    lax.fori_loop(0, 2, grads, 0)
+    heads(0, 2, grads)
     v_first(0)
     recv(("m", 0), mr1.at[0], dev_h1)
     mp[h2] = (widen(mp[h2]) + widen(mr1[0])).astype(BF16)
@@ -507,13 +505,11 @@
     a2a_recv(2, tb, rb)
     scan(rb, eb, True)
     a2a_start(3, eb, inb)
-    lax.fori_loop(2, 5, grads, 0)
-    v_relay(0)
+    heads(2, 4, grads)
     v_first(1)
-    lax.fori_loop(5, HEADS, grads, 0)
+    heads(4, HEADS, grads)
     wa[0, rows_a(a), :] = v_last(0).astype(BF16)
     send(("vz",), wa.at[0, rows_a(a)], xz, dev_z)
-    v_relay(1)
 
     a2a_recv(3, eb, inb)
     split(cb, sb, inb, back, lowb, 1)
@@ -538,7 +534,7 @@
         vg_ref[:, lanes(h)] = vg.astype(BF16)
         return carry
 
-    lax.fori_loop(0, HEADS, finish, 0)
+    heads(0, HEADS, finish)
     outs[1].start()
     outs[2].start()
 
@@ -587,10 +583,10 @@
     )
     whole = pltpu.VMEM((length, features), BF16)
     wide = pltpu.VMEM((length, features), F32)
-    piece = pltpu.VMEM((CHIPS, 40, DH), F32)
+    piece = pltpu.VMEM((CHIPS, 48, DH), BF16)
     state = pltpu.VMEM((CHIPS, 32, DH), BF16)
     scan = [
-        pltpu.VMEM((2 * CHIPS, 40, DH), F32), piece, piece, piece,
+        pltpu.VMEM((2 * CHIPS, 40, DH), F32), pltpu.VMEM((CHIPS, 40, DH), F32), piece, piece,
         state, state, state, pltpu.VMEM((2 * CHIPS, 32, DH), BF16),
     ]
 
@@ -631,8 +627,7 @@
             pltpu.VMEM((2, 2, 64, DOUT), BF16),
             pltpu.VMEM((2, 64, DOUT), F32),
             pltpu.VMEM((2, 64, DOUT), BF16),
-            pltpu.VMEM((2, 2, 16, HALF), BF16),
-            pltpu.VMEM((2, 2, 16, DOUT), BF16),
+            pltpu.VMEM((2, 3, 16, DOUT), BF16),
             pltpu.VMEM((16, DOUT), BF16),
             pltpu.VMEM((4, BLOCK, 768), BF16),
             pltpu.VMEM((BLOCK, 768), F32),

time: 86.5 us -> 83.4 us (0.964)
  the two profiles are of different devices: /device:TPU:2 before, /device:TPU:1 now
where the time goes in v3:
time: 83.4 us; the launch traced here: 81.9 us
  Pallas kernels  81.3 us (97%)
    pallas_call x1, Pallas kernels, shards(): pl.pallas_call(kernel, out_shape=shapes, in_specs=[hbm] * 6, out_specs=(h...  78.8 us
    pallas_call x1, Pallas kernels, shards(): pl.pallas_call(hand_out, out_shape=shapes, in_specs=[hbm] * 5, out_specs=...  2.44 us

profile of v3, /device:TPU:1, one launch (start us, length us, event | category | flops | bytes accessed | tf_op | source)
XLA Modules:
  0.0 81.9 jit_solution(17982809432948100325)
XLA Ops:
  0.6 78.8 %step.1 = (bf16[256,768]{1,0:T(8,128)(2,1)}, bf16[256,1024]{1,0:T(8,128)(2,1)}, bf16[256,1024]{1,0:T(8,128)(2,1)}, bf16[256,1024]{1,0:T(8,128)(2,1)}, f32[16,3072]{1,0:T(8,128)}) custom-call(bf16[256,1024]{1,0:T(8,128)(2,1)} %bitcast.12, bf16[256,1024]{1,0:T(8,128)(2,1)} %bitcast.13, bf16[256,1024]{1,0:T(8,128)(2,1)} %bitcast.14, f32[8,256]{1,0:T(8,128)} %bitcast.16, ...), custom_call_target="tpu_custom_call" | custom-call | tf_op jit(solution)/shard_map/step/pallas_call | solution.py:593
  79.5 2.4 %hand_out.1 = (bf16[256,768]{1,0:T(8,128)(2,1)}, bf16[256,1024]{1,0:T(8,128)(2,1)}, bf16[256,1024]{1,0:T(8,128)(2,1)}, bf16[256,1024]{1,0:T(8,128)(2,1)}, f32[16,3072]{1,0:T(8,128)}) custom-call(bf16[256,768]{1,0:T(8,128)(2,1)} %get-tuple-element.15.refs_0_, bf16[256,1024]{1,0:T(8,128)(2,1)} %get-tuple-element.16.refs_1_, ...), custom_call_target="tpu_custom_call" | custom-call | tf_op jit(solution)/shard_map/hand_out/pallas_call | solution.py:648

commit v4 on v3

--- a/solution.py
+++ b/solution.py
@@ -229,7 +229,7 @@
             out[j, 32:48, :] = three.astype(BF16)
             return carry
 
-        lax.fori_loop(0, CHIPS, go, 0)
+        lax.fori_loop(0, CHIPS, go, 0, unroll=2)
 
     def split(own, sib, got, out, out_sib, first):
         def go(j, carry):
@@ -240,7 +240,7 @@
             out_sib[j] = jnp.where(core == first, late, early).astype(BF16)
             return carry
 
-        lax.fori_loop(0, CHIPS, go, 0)
+        lax.fori_loop(0, CHIPS, go, 0, unroll=2)
 
     def a2a(n, src, dst, i, out):
         other = (chip + i) % CHIPS if out else (chip + CHIPS - i) % CHIPS
@@ -280,7 +280,7 @@
             decay = three[0:1] + three[5:6] + three[10:11]
             return state * decay + got[at_chip, 0:32, :].astype(F32)
 
-        lax.fori_loop(0, CHIPS, go, jnp.zeros((32, DH), F32))
+        lax.fori_loop(0, CHIPS, go, jnp.zeros((32, DH), F32), unroll=2)
 
     def state_of(buf, h):
         return buf[pl.ds(h * 4, 4)].reshape(DH, DH)
@@ -356,7 +356,7 @@
         attp[:, rows] = mm(att[...], pt[rows, :], NT).astype(BF16)
         return carry
 
-    lax.fori_loop(0, 4, turn, 0)
+    lax.fori_loop(0, 4, turn, 0, unroll=2)
     other_rows = pl.ds(pl.multiple_of((1 - core) * 512, 512), 512)
     send(("att",), att_t.at[other_rows], att_sib, dev_sib)
     for k in range(4):
@@ -387,7 +387,7 @@
             wp[zi, :, cols] = value.astype(BF16)
             return carry
 
-        lax.fori_loop(0, 12, go, 0)
+        lax.fori_loop(0, 12, go, 0, unroll=2)
 
     def w_first(zi):
         w_block(zi)
@@ -417,7 +417,7 @@
             wa[zi, :, cols] = total.astype(BF16)
             return carry
 
-        lax.fori_loop(0, 12, go, 0)
+        lax.fori_loop(0, 12, go, 0, unroll=2)
         for n, (a1, dev) in enumerate(((ao, dev_ao), (ap, dev_ap), (am, dev_am))):
             send(("v", zi, n), wa.at[zi, rows_a(a1)], ya.at[zi, n], dev)
 
@@ -427,11 +427,10 @@
         return wacc[zi, rows_a(a), :] + widen(ya[zi, 0]) + widen(ya[zi, 1]) + widen(ya[zi, 2])
 
     w_first(0)
-    w_first(1)
-
     for k in range(4):
         step_bo(1, k)
     sib_send(1, 3)
+    w_first(1)
     for zi in range(2):
         for k in range(4):
             sib_recv(zi, k)
@@ -443,7 +442,7 @@
             store(pl.ds(pl.multiple_of(n * 256, 256), 256), mm(attp[...], w, NN))
             return carry
 
-        lax.fori_loop(0, 3, go, 0)
+        lax.fori_loop(0, 3, go, 0, unroll=3)
 
     def store_at(dest):
         def store(cols, value):
@@ -465,7 +464,7 @@
         gh[:, cols] = mm(go_ref[...], rows, NT).astype(BF16)
         return carry
 
-    lax.fori_loop(0, 4, heads_grad, 0)
+    lax.fori_loop(0, 4, heads_grad, 0, unroll=2)
     by_head = []
     for n in range(4):
         by_head.append(mm(gh[...], pt[:, n * 256 : (n + 1) * 256], NN).astype(BF16))

time: 83.4 us -> 82.3 us (0.987); the launches traced: 81.9 us -> 82.2 us
  no operation moved by 1% of the time
where the time goes in v4:
time: 82.3 us; the launch traced here: 82.2 us
  Pallas kernels  81.5 us (99%)
    pallas_call x1, Pallas kernels, shards(): pl.pallas_call(kernel, out_shape=shapes, in_specs=[hbm] * 6, out_specs=(h...  79.1 us
    pallas_call x1, Pallas kernels, shards(): pl.pallas_call(hand_out, out_shape=shapes, in_specs=[hbm] * 5, out_specs=...  2.44 us

profile of v4, /device:TPU:1, one launch (start us, length us, event | category | flops | bytes accessed | tf_op | source)
XLA Modules:
  0.0 82.2 jit_solution(7477160609042557790)
XLA Ops:
  0.6 79.1 %step.1 = (bf16[256,768]{1,0:T(8,128)(2,1)}, bf16[256,1024]{1,0:T(8,128)(2,1)}, bf16[256,1024]{1,0:T(8,128)(2,1)}, bf16[256,1024]{1,0:T(8,128)(2,1)}, f32[16,3072]{1,0:T(8,128)}) custom-call(bf16[256,1024]{1,0:T(8,128)(2,1)} %bitcast.12, bf16[256,1024]{1,0:T(8,128)(2,1)} %bitcast.13, bf16[256,1024]{1,0:T(8,128)(2,1)} %bitcast.14, f32[8,256]{1,0:T(8,128)} %bitcast.16, ...), custom_call_target="tpu_custom_call" | custom-call | tf_op jit(solution)/shard_map/step/pallas_call | solution.py:592
  79.7 2.4 %hand_out.1 = (bf16[256,768]{1,0:T(8,128)(2,1)}, bf16[256,1024]{1,0:T(8,128)(2,1)}, bf16[256,1024]{1,0:T(8,128)(2,1)}, bf16[256,1024]{1,0:T(8,128)(2,1)}, f32[16,3072]{1,0:T(8,128)}) custom-call(bf16[256,768]{1,0:T(8,128)(2,1)} %get-tuple-element.15.refs_0_, bf16[256,1024]{1,0:T(8,128)(2,1)} %get-tuple-element.16.refs_1_, ...), custom_call_target="tpu_custom_call" | custom-call | tf_op jit(solution)/shard_map/hand_out/pallas_call | solution.py:647

commit v5 on v4

--- a/solution.py
+++ b/solution.py
@@ -497,10 +497,10 @@
         return carry
 
     heads(0, 2, grads)
-    v_first(0)
     recv(("m", 0), mr1.at[0], dev_h1)
     mp[h2] = (widen(mp[h2]) + widen(mr1[0])).astype(BF16)
     send(("m", 2), mp.at[h2], mr2, dev_h2)
+    v_first(0)
     a2a_recv(2, tb, rb)
     scan(rb, eb, True)
     a2a_start(3, eb, inb)

time: 82.3 us -> 80.6 us (0.979)
  Pallas kernels: 81.5 us -> 79.8 us
    pallas_call x1, Pallas kernels: 79.1 us -> 77.4 us  [shards(): pl.pallas_call(kernel, out_shape=shapes, in_specs=[hbm] * 6, out_specs=(h...]
where the time goes in v5:
time: 80.6 us; the launch traced here: 80.4 us
  Pallas kernels  79.8 us (99%)
    pallas_call x1, Pallas kernels, shards(): pl.pallas_call(kernel, out_shape=shapes, in_specs=[hbm] * 6, out_specs=(h...  77.4 us
    pallas_call x1, Pallas kernels, shards(): pl.pallas_call(hand_out, out_shape=shapes, in_specs=[hbm] * 5, out_specs=...  2.44 us

profile of v5, /device:TPU:1, one launch (start us, length us, event | category | flops | bytes accessed | tf_op | source)
XLA Modules:
  0.0 80.4 jit_solution(8202904280530722911)
XLA Ops:
  0.6 77.4 %step.1 = (bf16[256,768]{1,0:T(8,128)(2,1)}, bf16[256,1024]{1,0:T(8,128)(2,1)}, bf16[256,1024]{1,0:T(8,128)(2,1)}, bf16[256,1024]{1,0:T(8,128)(2,1)}, f32[16,3072]{1,0:T(8,128)}) custom-call(bf16[256,1024]{1,0:T(8,128)(2,1)} %bitcast.12, bf16[256,1024]{1,0:T(8,128)(2,1)} %bitcast.13, bf16[256,1024]{1,0:T(8,128)(2,1)} %bitcast.14, f32[8,256]{1,0:T(8,128)} %bitcast.16, ...), custom_call_target="tpu_custom_call" | custom-call | tf_op jit(solution)/shard_map/step/pallas_call | solution.py:592
  78.0 2.4 %hand_out.1 = (bf16[256,768]{1,0:T(8,128)(2,1)}, bf16[256,1024]{1,0:T(8,128)(2,1)}, bf16[256,1024]{1,0:T(8,128)(2,1)}, bf16[256,1024]{1,0:T(8,128)(2,1)}, f32[16,3072]{1,0:T(8,128)}) custom-call(bf16[256,768]{1,0:T(8,128)(2,1)} %get-tuple-element.15.refs_0_, bf16[256,1024]{1,0:T(8,128)(2,1)} %get-tuple-element.16.refs_1_, ...), custom_call_target="tpu_custom_call" | custom-call | tf_op jit(solution)/shard_map/hand_out/pallas_call | solution.py:647
